TPU v7x, 512 devices: a whole 4x4x16 slice. The times are simulated.
512 devices in a mesh: blk: 128 (over z, y, x_lo), rep: 4 (over x_hi, core).
Axes of the slice: x: 4 (x_hi: 2, x_lo: 2; x = x_hi * 2 + x_lo), y: 4, z: 16, core: 2. Of those that a mesh axis runs over, the one named last changes fastest.
Arguments:
- segment_ids: int32 [131072], P('rep'), parts along dimension 0, may hold values from 0 to 8191, as said below
- block_mask: int32 [512, 128], P('rep'), parts along dimension 0, may hold values from 0 to 1, as said below
- queries: bfloat16 [131072, 640], P(('rep', 'blk')), parts along dimension 0, may hold values from -256 to 256
- keys: bfloat16 [131072, 640], P(('rep', 'blk')), parts along dimension 0, may hold values from -8 to 8
- values: bfloat16 [131072, 640], P(('rep', 'blk')), parts along dimension 0, may hold values from -6 to 6
- tokens: bfloat16 [131072, 1280], P(('rep', 'blk')), parts along dimension 0, may hold values from -6 to 6
- out_weight: bfloat16 [640, 1280], replicated, may hold values from -6 to 6
- owners: int32 [32768], P(('rep', 'blk')), parts along dimension 0, may hold values from 0 to 127, as said below
- offsets: int32 [32768], P(('rep', 'blk')), parts along dimension 0, may hold values from 0 to 127, as said below
Outputs:
- received: bfloat16 [65536, 5120], P(('rep', 'blk')), parts along dimension 0
There are 4 independent parts, one for each index of `rep`. A program takes and returns all parts, laid end to end along the dimension named above; an argument that names none is the same for every part. Nothing has to cross between parts.
Inputs may be any that keep to these rules, and one draw needn't show every extreme that they name: `segment_ids`: never falls; every segment has a multiple of 4 patches and at most 768. `block_mask`: 1 exactly where the two blocks share a segment id. `owners`: the merged rows of one block name one owner at most 2 times; each owner is named by at most 128 rows. Rows that name the same owner have distinct offsets.
All inputs are finite; a program needn't handle non-finite values.
Results may differ from a plain program's by a relative error of at most 0.0065.
Values may be sent and summed in bfloat16 or wider, within the bound.
A program may use at most 64 MiB of HBM per device.

v0:
```python
import jax
import jax.numpy as jnp
from jax import lax
from jax.sharding import PartitionSpec as P

HEADS = 8
SPAN = 3


NEG = -1e30


def shifted(block, axis, distance):
    devices = range(lax.axis_size(axis))
    route = [(i - distance, i) for i in devices if i - distance in devices]
    return lax.ppermute(block, axis, route)


def attend(state, query_heads, key_part, value_part, allowed, scale):
    peak, total, accum = state
    scores = (
        jnp.einsum("rhd,khd->hrk", query_heads, key_part, preferred_element_type=jnp.float32)
        * scale
    )
    scores = jnp.where(allowed[None], scores, NEG)
    new_peak = jnp.maximum(peak, jnp.max(scores, axis=2, keepdims=True))
    weights = jnp.where(allowed[None], jnp.exp(scores - new_peak), 0.0)
    factor = jnp.exp(peak - new_peak)
    total = total * factor + jnp.sum(weights, axis=2, keepdims=True)
    accum = accum * factor + jnp.einsum(
        "hrk,khd->hrd", weights.astype(jnp.bfloat16), value_part, preferred_element_type=jnp.float32
    )
    return (new_peak, total, accum)


def block_flag(mask_row, column, nblocks):
    inside = (column >= 0) & (column < nblocks)
    return jnp.where(inside, mask_row[jnp.clip(column, 0, nblocks - 1)], 0)


def per_device(segment_ids, block_mask, queries, keys, values, tokens, out_weight, owners, offsets):
    rows = queries.shape[0]
    features = queries.shape[1]
    width = tokens.shape[1]
    hdim = features // HEADS
    nblocks = lax.axis_size("blk")
    block_index = lax.axis_index("blk")
    scale = 1.0 / jnp.sqrt(jnp.float32(hdim))
    pairs = (keys, values)
    fetched = {0: pairs}
    for dist in [d for d in range(-SPAN, SPAN + 1) if d != 0]:
        fetched[dist] = shifted((pairs[0], pairs[1]), "blk", -dist)
    mask_row = lax.dynamic_index_in_dim(block_mask, block_index, 0, keepdims=False)
    query_seg = lax.dynamic_slice_in_dim(segment_ids, block_index * rows, rows, 0)
    query_heads = queries.reshape(rows, HEADS, hdim)

    def seg_of(column):
        return lax.dynamic_slice_in_dim(
            segment_ids, jnp.clip(column, 0, nblocks - 1) * rows, rows, 0
        )

    state = (
        jnp.full((HEADS, rows, 1), NEG, jnp.float32),
        jnp.zeros((HEADS, rows, 1), jnp.float32),
        jnp.zeros((HEADS, rows, hdim), jnp.float32),
    )
    own_allowed = (query_seg[:, None] == query_seg[None, :]) & (
        block_flag(mask_row, block_index, nblocks) > 0
    )
    state = attend(
        state,
        query_heads,
        keys.reshape(rows, HEADS, hdim),
        values.reshape(rows, HEADS, hdim),
        own_allowed,
        scale,
    )
    for dist in range(1, SPAN + 1):
        lower = block_index - dist
        upper = block_index + dist
        flag_low = block_flag(mask_row, lower, nblocks)
        flag_high = block_flag(mask_row, upper, nblocks)
        key_cat = jnp.concatenate([fetched[-dist][0], fetched[dist][0]], axis=0).reshape(
            2 * rows, HEADS, hdim
        )
        value_cat = jnp.concatenate([fetched[-dist][1], fetched[dist][1]], axis=0).reshape(
            2 * rows, HEADS, hdim
        )
        seg_cat = jnp.concatenate([seg_of(lower), seg_of(upper)])
        flag_cat = jnp.concatenate(
            [jnp.full((rows,), flag_low, jnp.int32), jnp.full((rows,), flag_high, jnp.int32)]
        )
        allowed = (query_seg[:, None] == seg_cat[None, :]) & (flag_cat[None, :] > 0)
        state = lax.cond(
            flag_low + flag_high > 0,
            lambda carry: attend(carry, query_heads, key_cat, value_cat, allowed, scale),
            lambda carry: carry,
            state,
        )
    peak, total, accum = state
    attended = jnp.transpose(accum / total, (1, 0, 2)).reshape(rows, features).astype(jnp.bfloat16)
    mrows = rows // 4
    capacity = 2 * mrows
    pair_rows = max(2, 2 * mrows // nblocks)
    onehot = (owners[:, None] == jnp.arange(nblocks)[None, :]).astype(jnp.int32)
    ranks = jnp.sum((jnp.cumsum(onehot, axis=0) - 1) * onehot, axis=1)
    slot_index = owners * pair_rows + ranks
    outgoing_offsets = (
        jnp.full((nblocks * pair_rows,), capacity, jnp.int32).at[slot_index].set(offsets)
    )
    hidden = (
        tokens.astype(jnp.float32)
        + jnp.dot(attended, out_weight, preferred_element_type=jnp.float32)
    ).astype(jnp.bfloat16)
    merged = hidden.reshape(mrows, 4 * width)
    outgoing = jnp.zeros((nblocks * pair_rows, 4 * width), jnp.bfloat16).at[slot_index].set(merged)
    arrived, arrived_offsets = (
        lax.all_to_all(
            outgoing.reshape(nblocks, pair_rows, 4 * width),
            "blk",
            split_axis=0,
            concat_axis=0,
            tiled=True,
        ),
        lax.all_to_all(
            outgoing_offsets.reshape(nblocks, pair_rows),
            "blk",
            split_axis=0,
            concat_axis=0,
            tiled=True,
        ),
    )
    buffer = jnp.zeros((capacity, 4 * width), jnp.bfloat16)
    return buffer.at[arrived_offsets.reshape(-1)].set(arrived.reshape(-1, 4 * width), mode="drop")


def solution(mesh):
    placed = (
        P("rep"),
        P("rep", None),
        P(("rep", "blk"), None),
        P(("rep", "blk"), None),
        P(("rep", "blk"), None),
        P(("rep", "blk"), None),
        P(),
        P(("rep", "blk")),
        P(("rep", "blk")),
    )
    return jax.shard_map(
        per_device, mesh=mesh, in_specs=placed, out_specs=P(("rep", "blk"), None), check_vma=False
    )
```

profile of v0, /device:TPU:24, one launch (start us, length us, event | category | flops | bytes accessed | tf_op | source)
XLA Modules:
  0.0 280.0 jit_solution(10109195454156098866)
XLA Ops:
  0.0 3.5 %collective-permute-start = (bf16[256,640]{1,0:T(8,128)(2,1)}, bf16[256,640]{1,0:T(8,128)(2,1)S(1)}, u32[]{:S(2)}, u32[]{:S(2)}) collective-permute-start(bf16[256,640]{1,0:T(8,128)(2,1)} %param.18), channel_id=1, source_target_pairs={{0,4},{4,8},{8,12},{12,16},{16,20},{20,24},{24,28},{28,32},{32,36}... | collective-permute-start | bytes 983048 | tf_op jit(solution)/shard_map/ppermute | solution.py:16
  3.5 3.3 %collective-permute-start.1 = (bf16[256,640]{1,0:T(8,128)(2,1)}, bf16[256,640]{1,0:T(8,128)(2,1)S(1)}, u32[]{:S(2)}, u32[]{:S(2)}) collective-permute-start(bf16[256,640]{1,0:T(8,128)(2,1)} %param.18), channel_id=1, source_target_pairs={{4,0},{8,4},{12,8},{16,12},{20,16},{24,20},{28,24},{32,28},{36,32}... | collective-permute-start | bytes 983048 | tf_op jit(solution)/shard_map/ppermute | solution.py:16
  6.9 2.5 collective-permute-start.2
  9.4 4.2 %collective-permute-start.3 = (bf16[256,640]{1,0:T(8,128)(2,1)}, bf16[256,640]{1,0:T(8,128)(2,1)}, u32[]{:S(2)}, u32[]{:S(2)}) collective-permute-start(bf16[256,640]{1,0:T(8,128)(2,1)} %param.19), channel_id=1, source_target_pairs={{4,0},{8,4},{12,8},{16,12},{20,16},{24,20},{28,24},{32,28},{36,32}... | collective-permute-start | bytes 983048 | tf_op jit(solution)/shard_map/ppermute | solution.py:16
  13.6 1.9 copy.40
  15.5 7.7 %collective-permute-start.4 = (bf16[256,640]{0,1:T(8,128)(2,1)}, bf16[256,640]{0,1:T(8,128)(2,1)}, u32[]{:S(2)}, u32[]{:S(2)}) collective-permute-start(bf16[256,640]{0,1:T(8,128)(2,1)} %copy.40), channel_id=1, source_target_pairs={{0,8},{4,12},{8,16},{12,20},{16,24},{20,28},{24,32},{28,36},{32,40... | collective-permute-start | bytes 983048 | tf_op jit(solution)/shard_map/ppermute | solution.py:16
  27.2 20.2 %all-to-all-start = ((s32[128,1,2]{2,1,0:T(1,128)}), s32[128,1,2]{2,1,0:T(1,128)S(1)}, u32[]{:S(2)}, u32[]{:S(2)}) async-start(s32[128,1,2]{2,1,0:T(1,128)} %bitcast.16), calls=%async_computation | async-start | bytes 131072 | tf_op jit(solution)/shard_map/all_to_all | solution.py:125
  47.4 1.9 copy.41
  49.3 1.6 fusion.61
  53.8 1.5 fusion.41
  55.8 2.5 convolution_add_fusion.1
  62.5 2.8 collective-permute-start.5
  65.3 5.2 %collective-permute-start.6 = (bf16[256,640]{0,1:T(8,128)(2,1)}, bf16[256,640]{0,1:T(8,128)(2,1)}, u32[]{:S(2)}, u32[]{:S(2)}) collective-permute-start(bf16[256,640]{0,1:T(8,128)(2,1)} %copy.41), channel_id=1, source_target_pairs={{0,8},{4,12},{8,16},{12,20},{16,24},{20,28},{24,32},{28,36},{32,40... | collective-permute-start | bytes 983048 | tf_op jit(solution)/shard_map/ppermute | solution.py:16
  70.5 1.9 collective-permute-start.7
  73.8 6.9 %collective-permute-start.8 = (bf16[256,640]{0,1:T(8,128)(2,1)}, bf16[256,640]{0,1:T(8,128)(2,1)}, u32[]{:S(2)}, u32[]{:S(2)}) collective-permute-start(bf16[256,640]{0,1:T(8,128)(2,1)} %copy.40), channel_id=1, source_target_pairs={{0,12},{4,16},{8,20},{12,24},{16,28},{20,32},{24,36},{28,40},{32,4... | collective-permute-start | bytes 983048 | tf_op jit(solution)/shard_map/ppermute | solution.py:16
  80.7 1.9 collective-permute-start.9
  84.9 4.7 %conditional.3 = ((f32[8,256,1]{1,0,2:T(8,128)S(1)}, f32[8,256,1]{1,0,2:T(8,128)S(1)}, f32[8,256,80]{1,2,0:T(8,128)})) conditional(s32[]{:T(128)} %convert_element_type.43, (f32[8,256,1]{1,0,2:T(8,128)S(1)}, f32[8,256,1]{1,0,2:T(8,128)S(1)}, f32[8,256,80]{1,2,0:T(8,128)}) %tuple.25, (pred[256,512]{1,0:T(8,128)(4,1)S(1)}, ...), branch_computations={%region_5.6_spmd, %region_6.9_spmd} | conditional | flops 349509632 | bytes 23920756 | solution.py:94
  85.9 1.5 fusion.2
  87.4 1.3 fusion.6
  89.6 6.9 %collective-permute-start.10 = (bf16[256,640]{0,1:T(8,128)(2,1)}, bf16[256,640]{0,1:T(8,128)(2,1)}, u32[]{:S(2)}, u32[]{:S(2)}) collective-permute-start(bf16[256,640]{0,1:T(8,128)(2,1)} %copy.41), channel_id=1, source_target_pairs={{0,12},{4,16},{8,20},{12,24},{16,28},{20,32},{24,36},{28,40},{32,4... | collective-permute-start | bytes 983048 | tf_op jit(solution)/shard_map/ppermute | solution.py:16
  96.5 1.9 collective-permute-start.11
  100.8 5.0 %conditional.4 = ((f32[8,256,1]{1,0,2:T(8,128)S(1)}, f32[8,256,1]{1,0,2:T(8,128)S(1)}, f32[8,256,80]{1,2,0:T(8,128)})) conditional(s32[]{:T(128)} %convert_element_type.42, (f32[8,256,1]{1,0,2:T(8,128)S(1)}, f32[8,256,1]{1,0,2:T(8,128)S(1)}, f32[8,256,80]{1,2,0:T(8,128)}) %get-tuple-element.189, (s32[512]{0:T(512)S(1)}, s32[256,512]{1,0:T(8,128)S(1)}, ...), branch_computations={%region_9.10_spmd, %region_10.13_spmd} | conditional | flops 349772288 | bytes 21961824 | solution.py:94
  102.1 1.5 fusion.15
  103.7 1.3 fusion.19
  107.0 3.0 %collective-permute-done.11 = bf16[256,640]{0,1:T(8,128)(2,1)} collective-permute-done((bf16[256,640]{0,1:T(8,128)(2,1)}, bf16[256,640]{0,1:T(8,128)(2,1)}, u32[]{:S(2)}, u32[]{:S(2)}) %collective-permute-start.11) | collective-permute-done | bytes 327712 | tf_op jit(solution)/shard_map/ppermute | solution.py:16
  112.3 1.8 fusion.40
  114.5 3.4 %scatter_custom_fusion.1 = bf16[256,5120]{1,0:T(8,128)(2,1)} fusion(s32[64]{0:T(128)S(1)} %compare_select_fusion.1, bf16[64,5120]{1,0:T(8,128)(2,1)S(1)} %reshape.190, bf16[]{:T(256)} %constant.148.clone.1), kind=kCustom, calls=%fused_computation.60 | custom fusion | bytes 2621442 | tf_op jit(solution)/shard_map/scatter | solution.py:116
  117.9 6.3 %reshape.176 = bf16[128,2,5120]{2,1,0:T(2,128)(2,1)} reshape(bf16[256,5120]{1,0:T(8,128)(2,1)} %scatter_custom_fusion.1) | data formatting | bytes 5242880 | tf_op jit(solution)/shard_map/reshape | solution.py:119
  124.2 21.8 %all-to-all-start.1 = ((bf16[128,2,5120]{2,1,0:T(2,128)(2,1)}), bf16[128,2,5120]{2,1,0:T(2,128)(2,1)}, u32[]{:S(2)}, u32[]{:S(2)}) async-start(bf16[128,2,5120]{2,1,0:T(2,128)(2,1)} %reshape.176), calls=%async_computation.1 | async-start | bytes 5242880 | tf_op jit(solution)/shard_map/all_to_all | solution.py:118
  147.5 119.8 %all-to-all-done.1 = bf16[128,2,5120]{2,1,0:T(2,128)(2,1)} async-done(((bf16[128,2,5120]{2,1,0:T(2,128)(2,1)}), bf16[128,2,5120]{2,1,0:T(2,128)(2,1)}, u32[]{:S(2)}, u32[]{:S(2)}) %all-to-all-start.1) | async-done | bytes 2621472 | tf_op jit(solution)/shard_map/all_to_all | solution.py:118
  267.3 6.5 %reshape.198 = bf16[256,5120]{1,0:T(8,128)(2,1)} reshape(bf16[128,2,5120]{2,1,0:T(2,128)(2,1)} %all-to-all-done.1) | data formatting | bytes 5242880 | tf_op jit(solution)/shard_map/reshape | solution.py:134
  273.7 6.3 %scatter_custom_fusion.2 = bf16[128,5120]{1,0:T(8,128)(2,1)} fusion(s32[256]{0:T(256)S(1)} %bitcast.89, bf16[256,5120]{1,0:T(8,128)(2,1)} %reshape.198, bf16[]{:T(256)} %constant.148.clone.1), kind=kCustom, calls=%fused_computation.74 | custom fusion | bytes 1311232 | tf_op jit(solution)/shard_map/scatter | solution.py:134
  (74 shorter events, 21.8 us)
Async XLA Ops:
  0.0 112.3 %copy-start = (bf16[640,1280]{1,0:T(8,128)(2,1)S(1)}, bf16[640,1280]{1,0:T(8,128)(2,1)}, u32[]{:S(2)}) copy-start(bf16[640,1280]{1,0:T(8,128)(2,1)} %param.21) | copy-start | bytes 4915204
  0.0 62.5 %collective-permute-start = (bf16[256,640]{1,0:T(8,128)(2,1)}, bf16[256,640]{1,0:T(8,128)(2,1)S(1)}, u32[]{:S(2)}, u32[]{:S(2)}) collective-permute-start(bf16[256,640]{1,0:T(8,128)(2,1)} %param.18), channel_id=1, source_target_pairs={{0,4},{4,8},{8,12},{12,16},{16,20},{20,24},{24,28},{28,32},{32,36}... | collective-permute-start | bytes 983048 | tf_op jit(solution)/shard_map/ppermute | solution.py:16
  3.5 61.7 %collective-permute-start.1 = (bf16[256,640]{1,0:T(8,128)(2,1)}, bf16[256,640]{1,0:T(8,128)(2,1)S(1)}, u32[]{:S(2)}, u32[]{:S(2)}) collective-permute-start(bf16[256,640]{1,0:T(8,128)(2,1)} %param.18), channel_id=1, source_target_pairs={{4,0},{8,4},{12,8},{16,12},{20,16},{24,20},{28,24},{32,28},{36,32}... | collective-permute-start | bytes 983048 | tf_op jit(solution)/shard_map/ppermute | solution.py:16
  6.9 63.6 %collective-permute-start.2 = (bf16[256,640]{1,0:T(8,128)(2,1)}, bf16[256,640]{1,0:T(8,128)(2,1)S(1)}, u32[]{:S(2)}, u32[]{:S(2)}) collective-permute-start(bf16[256,640]{1,0:T(8,128)(2,1)} %param.19), channel_id=1, source_target_pairs={{0,4},{4,8},{8,12},{12,16},{16,20},{20,24},{24,28},{28,32},{32,36}... | collective-permute-start | bytes 983048 | tf_op jit(solution)/shard_map/ppermute | solution.py:16
  9.4 64.4 %collective-permute-start.3 = (bf16[256,640]{1,0:T(8,128)(2,1)}, bf16[256,640]{1,0:T(8,128)(2,1)}, u32[]{:S(2)}, u32[]{:S(2)}) collective-permute-start(bf16[256,640]{1,0:T(8,128)(2,1)} %param.19), channel_id=1, source_target_pairs={{4,0},{8,4},{12,8},{16,12},{20,16},{24,20},{28,24},{32,28},{36,32}... | collective-permute-start | bytes 983048 | tf_op jit(solution)/shard_map/ppermute | solution.py:16
  15.5 65.2 %collective-permute-start.4 = (bf16[256,640]{0,1:T(8,128)(2,1)}, bf16[256,640]{0,1:T(8,128)(2,1)}, u32[]{:S(2)}, u32[]{:S(2)}) collective-permute-start(bf16[256,640]{0,1:T(8,128)(2,1)} %copy.40), channel_id=1, source_target_pairs={{0,8},{4,12},{8,16},{12,20},{16,24},{20,28},{24,32},{28,36},{32,40... | collective-permute-start | bytes 983048 | tf_op jit(solution)/shard_map/ppermute | solution.py:16
  27.2 97.0 %all-to-all-start = ((s32[128,1,2]{2,1,0:T(1,128)}), s32[128,1,2]{2,1,0:T(1,128)S(1)}, u32[]{:S(2)}, u32[]{:S(2)}) async-start(s32[128,1,2]{2,1,0:T(1,128)} %bitcast.16), calls=%async_computation | async-start | bytes 131072 | tf_op jit(solution)/shard_map/all_to_all | solution.py:125
  62.5 27.1 %collective-permute-start.5 = (bf16[256,640]{0,1:T(8,128)(2,1)}, bf16[256,640]{0,1:T(8,128)(2,1)}, u32[]{:S(2)}, u32[]{:S(2)}) collective-permute-start(bf16[256,640]{0,1:T(8,128)(2,1)} %copy.40), channel_id=1, source_target_pairs={{8,0},{12,4},{16,8},{20,12},{24,16},{28,20},{32,24},{36,28},{40,32... | collective-permute-start | bytes 983048 | tf_op jit(solution)/shard_map/ppermute | solution.py:16
  65.3 5.2 %copy-start.9 = (bf16[256,640]{1,0:T(8,128)(2,1)}, bf16[256,640]{1,0:T(8,128)(2,1)S(1)}, u32[]{:S(2)}) copy-start(bf16[256,640]{1,0:T(8,128)(2,1)S(1)} %collective-permute-done.1) | copy-start | bytes 983044
  65.3 31.2 %collective-permute-start.6 = (bf16[256,640]{0,1:T(8,128)(2,1)}, bf16[256,640]{0,1:T(8,128)(2,1)}, u32[]{:S(2)}, u32[]{:S(2)}) collective-permute-start(bf16[256,640]{0,1:T(8,128)(2,1)} %copy.41), channel_id=1, source_target_pairs={{0,8},{4,12},{8,16},{12,20},{16,24},{20,28},{24,32},{28,36},{32,40... | collective-permute-start | bytes 983048 | tf_op jit(solution)/shard_map/ppermute | solution.py:16
  70.5 1.9 copy-start.8
  70.5 29.1 %collective-permute-start.7 = (bf16[256,640]{0,1:T(8,128)(2,1)}, bf16[256,640]{0,1:T(8,128)(2,1)}, u32[]{:S(2)}, u32[]{:S(2)}) collective-permute-start(bf16[256,640]{0,1:T(8,128)(2,1)} %copy.41), channel_id=1, source_target_pairs={{8,0},{12,4},{16,8},{20,12},{24,16},{28,20},{32,24},{36,28},{40,32... | collective-permute-start | bytes 983048 | tf_op jit(solution)/shard_map/ppermute | solution.py:16
  73.8 32.1 %collective-permute-start.8 = (bf16[256,640]{0,1:T(8,128)(2,1)}, bf16[256,640]{0,1:T(8,128)(2,1)}, u32[]{:S(2)}, u32[]{:S(2)}) collective-permute-start(bf16[256,640]{0,1:T(8,128)(2,1)} %copy.40), channel_id=1, source_target_pairs={{0,12},{4,16},{8,20},{12,24},{16,28},{20,32},{24,36},{28,40},{32,4... | collective-permute-start | bytes 983048 | tf_op jit(solution)/shard_map/ppermute | solution.py:16
  80.7 25.1 %collective-permute-start.9 = (bf16[256,640]{0,1:T(8,128)(2,1)}, bf16[256,640]{0,1:T(8,128)(2,1)}, u32[]{:S(2)}, u32[]{:S(2)}) collective-permute-start(bf16[256,640]{0,1:T(8,128)(2,1)} %copy.40), channel_id=1, source_target_pairs={{12,0},{16,4},{20,8},{24,12},{28,16},{32,20},{36,24},{40,28},{44,3... | collective-permute-start | bytes 983048 | tf_op jit(solution)/shard_map/ppermute | solution.py:16
  84.9 2.5 copy-start.1
  84.9 2.5 copy-start.2
  88.7 0.8 copy-start.3
  89.6 17.4 %collective-permute-start.10 = (bf16[256,640]{0,1:T(8,128)(2,1)}, bf16[256,640]{0,1:T(8,128)(2,1)}, u32[]{:S(2)}, u32[]{:S(2)}) collective-permute-start(bf16[256,640]{0,1:T(8,128)(2,1)} %copy.41), channel_id=1, source_target_pairs={{0,12},{4,16},{8,20},{12,24},{16,28},{20,32},{24,36},{28,40},{32,4... | collective-permute-start | bytes 983048 | tf_op jit(solution)/shard_map/ppermute | solution.py:16
  96.5 13.5 %collective-permute-start.11 = (bf16[256,640]{0,1:T(8,128)(2,1)}, bf16[256,640]{0,1:T(8,128)(2,1)}, u32[]{:S(2)}, u32[]{:S(2)}) collective-permute-start(bf16[256,640]{0,1:T(8,128)(2,1)} %copy.41), channel_id=1, source_target_pairs={{12,0},{16,4},{20,8},{24,12},{28,16},{32,20},{36,24},{40,28},{44,3... | collective-permute-start | bytes 983048 | tf_op jit(solution)/shard_map/ppermute | solution.py:16
  101.1 2.6 copy-start.4
  105.0 0.8 copy-start.5
  124.2 143.0 %all-to-all-start.1 = ((bf16[128,2,5120]{2,1,0:T(2,128)(2,1)}), bf16[128,2,5120]{2,1,0:T(2,128)(2,1)}, u32[]{:S(2)}, u32[]{:S(2)}) async-start(bf16[128,2,5120]{2,1,0:T(2,128)(2,1)} %reshape.176), calls=%async_computation.1 | async-start | bytes 5242880 | tf_op jit(solution)/shard_map/all_to_all | solution.py:118
where the time goes:
time: 281 us; the launch traced here: 280 us
  waiting for transfers between devices  123 us (44%)
  starting transfers between devices  90.9 us (32%)
  local copies, waits for them, and re-layouts  35.8 us (13%)
  other arithmetic  14.9 us (5%)
  matrix products  10.3 us (4%)
  between operations  5.05 us (2%)
    all_to_all x1, waiting for transfers between devices, per_device(): lax.all_to_all(outgoing.reshape(nblocks, pair_rows, 4 * width), 'blk', sp...  120 us
    ppermute x12, starting transfers between devices, shifted(): return lax.ppermute(block, axis, route)  48.9 us
    all_to_all x1, starting transfers between devices, per_device(): lax.all_to_all(outgoing.reshape(nblocks, pair_rows, 4 * width), 'blk', sp...  21.8 us
    all_to_all x1, starting transfers between devices, per_device(): lax.all_to_all(outgoing_offsets.reshape(nblocks, pair_rows), 'blk', split...  20.2 us
    reshape x1, local copies, waits for them, and re-layouts, per_device(): arrived.reshape(-1, 4 * width)  6.49 us
    reshape x1, local copies, waits for them, and re-layouts, per_device(): outgoing.reshape(nblocks, pair_rows, 4 * width)  6.28 us
    scatter x1, local copies, waits for them, and re-layouts, per_device(): buffer.at[arrived_offsets.reshape(-1)]  6.28 us
  transfers between devices with their start and end apart: 14, of which 2 were waited for; matrix products, arithmetic and copies ran while one was open for 16% of the time, Pallas kernels for 0%

commit v1 on v0

v1 whole, which is shorter than its diff:
```python
import functools

import jax
import jax.numpy as jnp
from jax import lax
from jax.experimental import pallas as pl
from jax.experimental.pallas import tpu as pltpu
from jax.sharding import PartitionSpec as P

HEADS = 8
SPAN = 3
NEG = -1e30
LANES = 128


def halo_kernel(nblk, k_ref, v_ref, kh, vh, ksend, vsend, krecv, vrecv):
    me = lax.axis_index("blk")
    rungs = nblk // 2
    rung, side = lax.div(me, 2), lax.rem(me, 2)
    up = lax.rem(rung + 1, rungs) * 2 + side
    down = lax.rem(rung + rungs - 1, rungs) * 2 + side
    across = rung * 2 + 1 - side
    far = lax.rem(rung + 1 - 2 * side + rungs, rungs) * 2 + side

    barrier = pltpu.get_barrier_semaphore()
    for other in (up, down, across):
        pl.semaphore_signal(barrier, inc=1, device_id={"blk": other}, device_id_type=pl.DeviceIdType.MESH)
    pl.semaphore_wait(barrier, 3)

    def send(src, dst, sends, recvs, number, slot, target):
        copy = pltpu.make_async_remote_copy(
            src_ref=src,
            dst_ref=dst.at[slot],
            send_sem=sends.at[number],
            recv_sem=recvs.at[slot],
            device_id={"blk": target},
            device_id_type=pl.DeviceIdType.MESH,
        )
        copy.start()
        return copy

    def arrived(dst, recvs, slot):
        pltpu.make_async_copy(dst.at[slot], dst.at[slot], recvs.at[slot]).wait()

    started = []
    started.append(send(v_ref, vh, vsend, vrecv, 0, 2 + side, across))
    started.append(send(k_ref, kh, ksend, krecv, 1, 1, up))
    started.append(send(k_ref, kh, ksend, krecv, 2, 4, down))
    started.append(send(k_ref, kh, ksend, krecv, 0, 2 + side, across))
    started.append(send(v_ref, vh, vsend, vrecv, 1, 1, up))
    started.append(send(v_ref, vh, vsend, vrecv, 2, 4, down))
    arrived(vh, vrecv, 3 - side)
    started.append(send(vh.at[3 - side], vh, vsend, vrecv, 3, 2 - 2 * side, up))
    started.append(send(vh.at[3 - side], vh, vsend, vrecv, 4, 5 - 2 * side, down))
    arrived(kh, krecv, 1)
    started.append(send(kh.at[1], kh, ksend, krecv, 3, 2 * side, across))
    arrived(kh, krecv, 4)
    started.append(send(kh.at[4], kh, ksend, krecv, 4, 3 + 2 * side, across))
    arrived(kh, krecv, 2 - 2 * side)
    arrived(kh, krecv, 5 - 2 * side)
    started.append(send(kh.at[2 + side], kh, ksend, krecv, 5, 5 * side, far))
    arrived(vh, vrecv, 2 - 2 * side)
    arrived(vh, vrecv, 5 - 2 * side)
    started.append(send(vh.at[2 + side], vh, vsend, vrecv, 5, 5 * side, far))
    arrived(kh, krecv, 3 - side)
    arrived(vh, vrecv, 1)
    arrived(vh, vrecv, 4)
    arrived(kh, krecv, 5 * side)
    arrived(vh, vrecv, 5 * side)
    for copy in started:
        copy.wait_send()


def halo(keys, values, nblk):
    rows, features = keys.shape
    shape = jax.ShapeDtypeStruct((2 * SPAN, rows, features), keys.dtype)
    return pl.pallas_call(
        functools.partial(halo_kernel, nblk),
        out_shape=(shape, shape),
        in_specs=[pl.BlockSpec(memory_space=pl.ANY)] * 2,
        out_specs=(pl.BlockSpec(memory_space=pl.ANY),) * 2,
        scratch_shapes=[pltpu.SemaphoreType.DMA((6,))] * 4,
        compiler_params=pltpu.CompilerParams(collective_id=0, has_side_effects=True),
    )(keys, values)


def to_column(row):
    size = row.shape[1]
    diagonal = lax.broadcasted_iota(jnp.int32, (size, size), 0) == lax.broadcasted_iota(
        jnp.int32, (size, size), 1
    )
    return jnp.sum(jnp.where(diagonal, row, 0), axis=1, keepdims=True)


def attend_kernel(
    here, q_ref, k_ref, v_ref, kh, vh, seg_ref, mask_ref, tok_ref, w_ref, route_ref, out_ref, att
):
    rows, features = q_ref.shape
    nblk = seg_ref.shape[0]
    width = tok_ref.shape[1]
    hdim = features // HEADS
    block = here[0]
    scale = 1.0 / jnp.sqrt(jnp.float32(hdim))
    query_seg = to_column(seg_ref[pl.ds(block, 1), :])
    mask_row = mask_ref[pl.ds(block, 1), :]
    columns = lax.broadcasted_iota(jnp.int32, mask_row.shape, 1)
    key_segs, sources = [], []
    for dist in range(-SPAN, SPAN + 1):
        column = block + dist
        flag = jnp.sum(jnp.where(columns == column, mask_row, 0), axis=1, keepdims=True)
        ids = seg_ref[pl.ds(jnp.clip(column, 0, nblk - 1), 1), :]
        key_segs.append(jnp.where(flag > 0, ids, -1))
        if dist == 0:
            sources.append((k_ref, v_ref))
        else:
            slot = dist + SPAN - (1 if dist > 0 else 0)
            sources.append((kh.at[slot], vh.at[slot]))
    for head in range(HEADS):
        first, last = head * hdim, (head + 1) * hdim
        low = first // LANES * LANES
        high = -(-last // LANES) * LANES
        lane = lax.broadcasted_iota(jnp.int32, (rows, high - low), 1) + low
        mine = (lane >= first) & (lane < last)
        query = jnp.where(mine, q_ref[:, low:high], jnp.bfloat16(0))
        scores = []
        for (key, _), key_seg in zip(sources, key_segs):
            part = lax.dot_general(
                query, key[:, low:high], (((1,), (1,)), ((), ())), preferred_element_type=jnp.float32
            )
            scores.append(jnp.where(query_seg == key_seg, part, NEG))
        peak = functools.reduce(jnp.maximum, scores)
        peak = jnp.max(peak, axis=1, keepdims=True)
        total = jnp.zeros((rows, 1), jnp.float32)
        mixed = jnp.zeros((rows, high - low), jnp.float32)
        for (_, value), part in zip(sources, scores):
            weights = jnp.exp((part - peak) * scale)
            total = total + jnp.sum(weights, axis=1, keepdims=True)
            mixed = mixed + jnp.dot(
                weights.astype(jnp.bfloat16), value[:, low:high], preferred_element_type=jnp.float32
            )
        att[:, low:high] = jnp.where(mine, mixed / total, att[:, low:high])
    hidden = (
        tok_ref[...].astype(jnp.float32)
        + jnp.dot(att[...].astype(jnp.bfloat16), w_ref[...], preferred_element_type=jnp.float32)
    ).astype(jnp.bfloat16)
    owner_row = route_ref[0:1, :]
    owner_col = to_column(owner_row)
    down = lax.broadcasted_iota(jnp.int32, (rows, rows), 0)
    right = lax.broadcasted_iota(jnp.int32, (rows, rows), 1)
    earlier = (owner_col == owner_row) & (down < right // 4 * 4) & (down % 4 == 0)
    rank = jnp.sum(earlier.astype(jnp.int32), axis=0, keepdims=True)
    slot = 2 * owner_row + rank
    hit = down == slot
    for quarter in range(4):
        pick = (hit & (right % 4 == quarter)).astype(jnp.float32)
        if quarter == 0:
            offset = jnp.sum(pick * route_ref[1:2, :].astype(jnp.float32), axis=1, keepdims=True)
            used = jnp.sum(pick, axis=1, keepdims=True)
            offset = jnp.where(used > 0, offset, 2.0 * nblk)
            out_ref[:, 4 * width :] = jnp.broadcast_to(offset, (rows, LANES)).astype(jnp.bfloat16)
        out_ref[:, quarter * width : (quarter + 1) * width] = jnp.dot(
            pick.astype(jnp.bfloat16), hidden, preferred_element_type=jnp.float32
        ).astype(jnp.bfloat16)


def place_kernel(in_ref, out_ref):
    slots = in_ref.shape[0]
    rows, width = out_ref.shape
    tag = in_ref[:, width:].astype(jnp.float32)[:, 0:1]
    down = lax.broadcasted_iota(jnp.int32, (slots, slots), 0)
    right = lax.broadcasted_iota(jnp.int32, (slots, slots), 1)
    tag = jnp.sum(jnp.where(down == right, tag, 0.0), axis=0, keepdims=True)
    spot = lax.broadcasted_iota(jnp.int32, (rows, slots), 0).astype(jnp.float32)
    pick = jnp.where(spot == tag, 1.0, 0.0).astype(jnp.bfloat16)
    step = width // 4
    for start in range(0, width, step):
        out_ref[:, start : start + step] = jnp.dot(
            pick, in_ref[:, start : start + step], preferred_element_type=jnp.float32
        ).astype(jnp.bfloat16)


def per_device(segment_ids, block_mask, queries, keys, values, tokens, out_weight, owners, offsets):
    rows = queries.shape[0]
    width = tokens.shape[1]
    nblk = lax.axis_size("blk")
    mrows = rows // 4
    capacity = 2 * mrows
    wide = 4 * width + LANES
    key_halo, value_halo = halo(keys, values, nblk)
    here = lax.axis_index("blk").reshape(1)
    route = jnp.broadcast_to(jnp.stack([owners, offsets])[:, :, None], (2, mrows, 4)).reshape(2, rows)
    vmem = pl.BlockSpec(memory_space=pltpu.VMEM)
    outgoing = pl.pallas_call(
        attend_kernel,
        out_shape=jax.ShapeDtypeStruct((2 * nblk, wide), jnp.bfloat16),
        in_specs=[pl.BlockSpec(memory_space=pltpu.SMEM)] + [vmem] * 10,
        out_specs=vmem,
        scratch_shapes=[pltpu.VMEM(queries.shape, jnp.float32)],
        compiler_params=pltpu.CompilerParams(vmem_limit_bytes=48 * 2**20),
    )(
        here,
        queries,
        keys,
        values,
        key_halo,
        value_halo,
        segment_ids.reshape(nblk, rows),
        block_mask,
        tokens,
        out_weight,
        route,
    )
    arrived = lax.all_to_all(
        outgoing.reshape(nblk, 2, wide), "blk", split_axis=0, concat_axis=0, tiled=True
    )
    return pl.pallas_call(
        place_kernel,
        out_shape=jax.ShapeDtypeStruct((capacity, 4 * width), jnp.bfloat16),
        in_specs=[vmem],
        out_specs=vmem,
    )(arrived.reshape(2 * nblk, wide))


def solution(mesh):
    placed = (
        P("rep"),
        P("rep", None),
        P(("rep", "blk"), None),
        P(("rep", "blk"), None),
        P(("rep", "blk"), None),
        P(("rep", "blk"), None),
        P(),
        P(("rep", "blk")),
        P(("rep", "blk")),
    )
    return jax.shard_map(
        per_device, mesh=mesh, in_specs=placed, out_specs=P(("rep", "blk"), None), check_vma=False
    )
```

time: 281 us -> 229 us (0.81)
  blocking collectives: 0 us -> 145 us
  waiting for transfers between devices: 123 us -> 0 us
  starting transfers between devices: 90.9 us -> 0 us
  Pallas kernels: 0 us -> 62.1 us
  local copies, waits for them, and re-layouts: 35.8 us -> 20.7 us
  other arithmetic: 14.9 us -> 0.68 us
  matrix products: 10.3 us -> 0 us
  between operations: 5.05 us -> 0.04 us
    all_to_all x0 -> x1, blocking collectives: none -> 145 us  [per_device(): lax.all_to_all(outgoing.reshape(nblk, 2, wide), 'blk', split_axis=0, conc...]
    all_to_all x2 -> x0, waiting for transfers between devices: 120 us -> none  [the longest x1 120 us: per_device(): lax.all_to_all(outgoing.reshape(nblocks, pair_rows, 4 * width), 'blk', sp...]
    pallas_call x0 -> x3, Pallas kernels: none -> 62.1 us  [the longest x1 47.5 us: halo(): pl.pallas_call(functools.partial(halo_kernel, nblk), out_shape=(shape, sh...]
    ppermute x12 -> x0, starting transfers between devices: 48.9 us -> none  [shifted(): return lax.ppermute(block, axis, route)]
    all_to_all x2 -> x0, starting transfers between devices: 42 us -> none  [the longest x1 21.8 us: per_device(): lax.all_to_all(outgoing.reshape(nblocks, pair_rows, 4 * width), 'blk', sp...]
    scatter x3 -> x0, local copies, waits for them, and re-layouts: 10.6 us -> none  [the longest x1 6.28 us: per_device(): buffer.at[arrived_offsets.reshape(-1)]]
    dot_general x7 -> x0, matrix products: 10.3 us -> none  [the longest x3 5.07 us: attend(): jnp.einsum('hrk,khd->hrd', weights.astype(jnp.bfloat16), value_part, pref...]
    concatenate x9 -> x0, other arithmetic: 6.65 us -> none  [the longest x3 3.36 us: per_device(): jnp.concatenate([fetched[-dist][1], fetched[dist][1]], axis=0)]
  transfers between devices with their start and end apart: 14 -> 0, of which waited for: 2 -> 0; matrix products, arithmetic and copies ran while one was open for 16% -> 0% of each run, Pallas kernels for 0% -> 0%
where the time goes in v1:
time: 229 us
  blocking collectives  145 us (63%)
  Pallas kernels  62.1 us (27%)
  local copies, waits for them, and re-layouts  20.7 us (9%)
    all_to_all x1, blocking collectives, per_device(): lax.all_to_all(outgoing.reshape(nblk, 2, wide), 'blk', split_axis=0, conc...  145 us
    pallas_call x1, Pallas kernels, halo(): pl.pallas_call(functools.partial(halo_kernel, nblk), out_shape=(shape, sh...  47.5 us
    pallas_call x1, Pallas kernels, per_device(): pl.pallas_call(attend_kernel, out_shape=jax.ShapeDtypeStruct((2 * nblk, w...  11.2 us
    unnamed x14, local copies, waits for them, and re-layouts  7.81 us
    reshape x1, local copies, waits for them, and re-layouts, per_device(): arrived.reshape(2 * nblk, wide)  6.57 us
    reshape x1, local copies, waits for them, and re-layouts, per_device(): outgoing.reshape(nblk, 2, wide)  5.2 us

profile of v1, /device:TPU:24, one launch (start us, length us, event | category | flops | bytes accessed | tf_op | source)
XLA Modules:
  0.0 228.6 jit_solution(4571963429026682755)
XLA Ops:
  0.0 0.7 pad_add_fusion
  0.7 0.1 broadcast_in_dim.2
  0.8 0.1 reshape.18.route_ref
  0.9 0.9 reshape.17.seg_ref
  1.8 47.5 %shard_map.91 = (bf16[6,256,640]{2,1,0:T(8,128)(2,1)}, bf16[6,256,640]{2,1,0:T(8,128)(2,1)}) custom-call(bf16[256,640]{1,0:T(8,128)(2,1)} %k_ref.3, bf16[256,640]{1,0:T(8,128)(2,1)} %v_ref.3), custom_call_target="tpu_custom_call" | custom-call | tf_op jit(solution)/shard_map/pallas_call | solution.py:77
  49.3 0.0 copy-start
  49.3 1.5 copy-done
  50.8 0.0 copy-start.1
  50.9 1.4 copy-done.1
  52.3 0.0 copy-start.2
  52.3 1.0 copy-done.2
  53.3 0.0 copy-start.3
  53.3 1.0 copy-done.3
  54.2 0.0 copy-start.4
  54.2 1.1 copy-done.4
  55.3 0.0 copy-start.5
  55.3 1.0 copy-done.5
  56.3 0.0 copy-start.6
  56.3 0.8 copy-done.6
  57.1 11.2 %shard_map.92 = bf16[256,5248]{1,0:T(8,128)(2,1)} custom-call(s32[1]{0:T(128)} %bitcast.here, bf16[256,640]{1,0:T(8,128)(2,1)S(1)} %copy-done.5, bf16[256,640]{1,0:T(8,128)(2,1)S(1)} %copy-done.2, bf16[256,640]{1,0:T(8,128)(2,1)S(1)} %copy-done.3, bf16[6,256,640]{2,1,0:T(8,128)(2,1)S(1)} %copy-done, bf16[6,256,640]{2,1,0:T(8,128)(2,1)} %get-tuple-element.8.vh, ...), custom_call_target="tpu_custom_call" | custom-call | tf_op jit(solution)/shard_map/pallas_call | solution.py:193
  68.3 5.2 %reshape.19 = bf16[128,2,5248]{2,1,0:T(2,128)(2,1)S(1)} reshape(bf16[256,5248]{1,0:T(8,128)(2,1)} %shard_map.92) | data formatting | bytes 5373952 | tf_op jit(solution)/shard_map/reshape | solution.py:214
  73.5 145.1 %all_to_all.5 = bf16[128,2,5248]{2,1,0:T(2,128)(2,1)} all-to-all(bf16[128,2,5248]{2,1,0:T(2,128)(2,1)S(1)} %reshape.19), channel_id=1, replica_groups=mesh['blk'=128,'rep'=4] {'blk'}, dimensions={0} | all-to-all | bytes 5373952 | tf_op jit(solution)/shard_map/all_to_all | solution.py:213
  218.6 6.6 %reshape.20.in_ref = bf16[256,5248]{1,0:T(8,128)(2,1)} reshape(bf16[128,2,5248]{2,1,0:T(2,128)(2,1)} %all_to_all.5) | data formatting | bytes 5373952 | tf_op jit(solution)/shard_map/reshape | solution.py:221
  225.2 3.4 %shard_map.93 = bf16[128,5120]{1,0:T(8,128)(2,1)} custom-call(bf16[256,5248]{1,0:T(8,128)(2,1)} %reshape.20.in_ref), custom_call_target="tpu_custom_call" | custom-call | tf_op jit(solution)/shard_map/pallas_call | solution.py:216
Async XLA Ops:
  49.3 1.5 copy-start
  50.8 1.4 copy-start.1
  52.3 1.0 copy-start.2
  53.3 1.0 copy-start.3
  54.2 1.1 copy-start.4
  55.3 1.0 copy-start.5
  56.3 0.8 copy-start.6

commit v2 on v1

--- a/solution.py
+++ b/solution.py
@@ -11,6 +11,9 @@
 SPAN = 3
 NEG = -1e30
 LANES = 128
+PLANE = 8
+REACH = 4
+CHUNKS = 4
 
 
 def halo_kernel(nblk, k_ref, v_ref, kh, vh, ksend, vsend, krecv, vrecv):
@@ -150,33 +153,219 @@
     earlier = (owner_col == owner_row) & (down < right // 4 * 4) & (down % 4 == 0)
     rank = jnp.sum(earlier.astype(jnp.int32), axis=0, keepdims=True)
     slot = 2 * owner_row + rank
-    hit = down == slot
+    mrows = rows // 4
+    merged = lax.broadcasted_iota(jnp.int32, (mrows, rows), 0)
+    source = lax.broadcasted_iota(jnp.int32, (mrows, rows), 1)
+    lane = lax.broadcasted_iota(jnp.int32, (mrows, LANES), 1)
     for quarter in range(4):
-        pick = (hit & (right % 4 == quarter)).astype(jnp.float32)
+        pick = source == 4 * merged + quarter
         if quarter == 0:
-            offset = jnp.sum(pick * route_ref[1:2, :].astype(jnp.float32), axis=1, keepdims=True)
-            used = jnp.sum(pick, axis=1, keepdims=True)
-            offset = jnp.where(used > 0, offset, 2.0 * nblk)
-            out_ref[:, 4 * width :] = jnp.broadcast_to(offset, (rows, LANES)).astype(jnp.bfloat16)
-        out_ref[:, quarter * width : (quarter + 1) * width] = jnp.dot(
-            pick.astype(jnp.bfloat16), hidden, preferred_element_type=jnp.float32
+            offset = jnp.sum(jnp.where(pick, route_ref[1:2, :], 0), axis=1, keepdims=True)
+            code = jnp.sum(jnp.where(pick, slot, 0), axis=1, keepdims=True)
+            tags = jnp.where(lane < LANES // 2, offset + 1, code + 1)
+            out_ref[:, :LANES] = tags.astype(jnp.float32).astype(jnp.bfloat16)
+        start = LANES + quarter * width
+        out_ref[:, start : start + width] = jnp.dot(
+            pick.astype(jnp.float32).astype(jnp.bfloat16), hidden, preferred_element_type=jnp.float32
         ).astype(jnp.bfloat16)
 
 
-def place_kernel(in_ref, out_ref):
-    slots = in_ref.shape[0]
-    rows, width = out_ref.shape
-    tag = in_ref[:, width:].astype(jnp.float32)[:, 0:1]
-    down = lax.broadcasted_iota(jnp.int32, (slots, slots), 0)
-    right = lax.broadcasted_iota(jnp.int32, (slots, slots), 1)
-    tag = jnp.sum(jnp.where(down == right, tag, 0.0), axis=0, keepdims=True)
-    spot = lax.broadcasted_iota(jnp.int32, (rows, slots), 0).astype(jnp.float32)
-    pick = jnp.where(spot == tag, 1.0, 0.0).astype(jnp.bfloat16)
-    step = width // 4
-    for start in range(0, width, step):
-        out_ref[:, start : start + step] = jnp.dot(
-            pick, in_ref[:, start : start + step], preferred_element_type=jnp.float32
+def to_row(column):
+    size = column.shape[0]
+    diagonal = lax.broadcasted_iota(jnp.int32, (size, size), 0) == lax.broadcasted_iota(
+        jnp.int32, (size, size), 1
+    )
+    return jnp.sum(jnp.where(diagonal, column, 0.0), axis=0, keepdims=True)
+
+
+def codes_of(tags):
+    return to_row(tags.astype(jnp.float32)[:, LANES // 2 : LANES // 2 + 1])
+
+
+def as_onehot(hit):
+    return jnp.where(hit, 1.0, 0.0).astype(jnp.bfloat16)
+
+
+def pick_rows(onehot, rows):
+    return jnp.dot(onehot, rows, preferred_element_type=jnp.float32)
+
+
+def route_kernel(
+    nblk, r_ref, out_ref, near, comp, far, ordered, landed, nsend, nrecv, fsend, frecv, psend, precv
+):
+    me = lax.axis_index("blk")
+    planes = nblk // PLANE
+    plane, spot = lax.div(me, PLANE), lax.rem(me, PLANE)
+    mrows, wide = r_ref.shape
+    per = 2 * PLANE
+    step = (wide - LANES) // CHUNKS
+    chunks = [(0, LANES + step)] + [(LANES + c * step, step) for c in range(1, CHUNKS)]
+
+    def along(distance):
+        return lax.rem(plane + distance + planes, planes) * PLANE + spot
+
+    def within(distance):
+        return plane * PLANE + lax.rem(spot + distance, PLANE)
+
+    barrier = pltpu.get_barrier_semaphore()
+    peers = [along(d) for k in range(1, REACH + 1) for d in (k, -k)]
+    peers += [within(d) for d in range(1, PLANE)]
+    for other in peers:
+        pl.semaphore_signal(barrier, inc=1, device_id={"blk": other}, device_id_type=pl.DeviceIdType.MESH)
+    pl.semaphore_wait(barrier, len(peers))
+
+    started = []
+
+    def send(src, dst, sends, recvs, number, target):
+        copy = pltpu.make_async_remote_copy(
+            src_ref=src,
+            dst_ref=dst,
+            send_sem=sends.at[number],
+            recv_sem=recvs.at[number],
+            device_id={"blk": target},
+            device_id_type=pl.DeviceIdType.MESH,
+        )
+        copy.start()
+        started.append(copy)
+        return copy
+
+    def near_at(way, hop):
+        return (way * REACH + hop - 1) * mrows
+
+    def forward(way, hop, chunk):
+        begin, size = chunks[chunk]
+        cols = pl.ds(begin, size)
+        src = r_ref.at[:, cols] if hop == 1 else near.at[pl.ds(near_at(way, hop - 1), mrows), cols]
+        return send(
+            src,
+            near.at[pl.ds(near_at(way, hop), mrows), cols],
+            nsend,
+            nrecv,
+            (way * REACH + hop - 1) * CHUNKS + chunk,
+            along(1 - 2 * way),
+        )
+
+    hops = {}
+    for chunk in range(CHUNKS):
+        for way in range(2):
+            hops[way, 1, chunk] = forward(way, 1, chunk)
+    for hop in range(1, REACH):
+        for chunk in range(CHUNKS):
+            for way in range(2):
+                hops[way, hop, chunk].wait_recv()
+                hops[way, hop + 1, chunk] = forward(way, hop + 1, chunk)
+
+    def far_at(way, ahead):
+        return (way * (REACH - 1) + ahead - 1) * per if ahead < REACH else 2 * (REACH - 1) * per
+
+    relays, onehots = {}, {}
+    for chunk, (begin, size) in enumerate(chunks):
+        for way in range(2):
+            hops[way, REACH, chunk].wait_recv()
+            held = near_at(way, REACH)
+            if chunk == 0:
+                code = codes_of(near[held : held + mrows, :LANES])
+                index = lax.broadcasted_iota(jnp.int32, (REACH * per, mrows), 0)
+                ahead = index // per + 1
+                goal = plane + (ahead if way == 0 else planes - ahead)
+                goal = jnp.where(goal >= planes, goal - planes, goal)
+                want = goal * per + index % per + 1
+                onehots[way] = as_onehot(code == want.astype(jnp.float32))
+            comp[way * REACH * per : (way + 1) * REACH * per, begin : begin + size] = pick_rows(
+                onehots[way], near[held : held + mrows, begin : begin + size]
+            ).astype(jnp.bfloat16)
+            for ahead in range(REACH, 0, -1):
+                if ahead == REACH and chunk * 2 // CHUNKS != way:
+                    continue
+                relays[way, ahead, chunk] = send(
+                    comp.at[pl.ds((way * REACH + ahead - 1) * per, per), pl.ds(begin, size)],
+                    far.at[pl.ds(far_at(way, ahead), per), pl.ds(begin, size)],
+                    fsend,
+                    frecv,
+                    (way * REACH + ahead - 1) * CHUNKS + chunk,
+                    along(ahead - 2 * way * ahead),
+                )
+
+    slots = per * planes
+    each = slots // PLANE
+
+    def wanted(columns):
+        index = lax.broadcasted_iota(jnp.int32, (slots, columns), 0)
+        column = lax.broadcasted_iota(jnp.int32, (slots, columns), 1)
+        return index % each // 2, index // each * 2 + index % 2, column
+
+    base = plane * per + 1
+    group, local, column = wanted(mrows)
+    code = codes_of(r_ref[:, :LANES])
+    own_hot = as_onehot((group == 0) & (code == (local + base).astype(jnp.float32)))
+    group, local, column = wanted(2 * REACH * mrows)
+    code = codes_of(near[:, :LANES])
+    near_hot = as_onehot(
+        (group == 1 + column // mrows) & (code == (local + base).astype(jnp.float32))
+    )
+    group, local, column = wanted(far.shape[0])
+    far_hot = as_onehot((group == 1 + 2 * REACH + column // per) & (local == column % per))
+
+    spread = {}
+    mine = pl.ds(pl.multiple_of(spot * each, each), each)
+    for chunk, (begin, size) in enumerate(chunks):
+        cols = slice(begin, begin + size)
+        found = pick_rows(own_hot, r_ref[:, cols]) + pick_rows(near_hot, near[:, cols])
+        for way in range(2):
+            for ahead in range(1, REACH + 1):
+                if (way, ahead, chunk) in relays:
+                    relays[way, ahead, chunk].wait_recv()
+        ordered[:, cols] = (found + pick_rows(far_hot, far[:, cols])).astype(jnp.bfloat16)
+        for distance in range(1, PLANE):
+            theirs = pl.ds(pl.multiple_of(lax.rem(spot + distance, PLANE) * each, each), each)
+            spread[distance, chunk] = send(
+                ordered.at[theirs, pl.ds(begin, size)],
+                landed.at[mine, pl.ds(begin, size)],
+                psend,
+                precv,
+                (distance - 1) * CHUNKS + chunk,
+                within(distance),
+            )
+        landed[mine, cols] = ordered[mine, cols]
+
+    for chunk, (begin, size) in enumerate(chunks):
+        for distance in range(1, PLANE):
+            spread[distance, chunk].wait_recv()
+        if chunk == 0:
+            tag = to_row(landed[:, :LANES].astype(jnp.float32)[:, 0:1])
+            index = lax.broadcasted_iota(jnp.int32, (out_ref.shape[0], slots), 0) + 1
+            place = as_onehot(index.astype(jnp.float32) == tag)
+            begin, size = begin + LANES, size - LANES
+        out_ref[:, begin - LANES : begin - LANES + size] = pick_rows(
+            place, landed[:, begin : begin + size]
         ).astype(jnp.bfloat16)
+    for copy in started:
+        copy.wait_send()
+
+
+def route_rows(rows, nblk, capacity):
+    mrows, wide = rows.shape
+    per = 2 * PLANE
+    vmem = pl.BlockSpec(memory_space=pltpu.VMEM)
+    dma = pltpu.SemaphoreType.DMA
+    return pl.pallas_call(
+        functools.partial(route_kernel, nblk),
+        out_shape=jax.ShapeDtypeStruct((capacity, wide - LANES), rows.dtype),
+        in_specs=[vmem],
+        out_specs=vmem,
+        scratch_shapes=[
+            pltpu.VMEM((2 * REACH * mrows, wide), rows.dtype),
+            pltpu.VMEM((2 * REACH * per, wide), rows.dtype),
+            pltpu.VMEM(((2 * REACH - 1) * per, wide), rows.dtype),
+            pltpu.VMEM((2 * nblk, wide), rows.dtype),
+            pltpu.VMEM((2 * nblk, wide), rows.dtype),
+        ]
+        + [dma((2 * REACH * CHUNKS,))] * 4
+        + [dma(((PLANE - 1) * CHUNKS,))] * 2,
+        compiler_params=pltpu.CompilerParams(
+            collective_id=1, has_side_effects=True, vmem_limit_bytes=48 * 2**20
+        ),
+    )(rows)
 
 
 def per_device(segment_ids, block_mask, queries, keys, values, tokens, out_weight, owners, offsets):
@@ -192,7 +381,7 @@
     vmem = pl.BlockSpec(memory_space=pltpu.VMEM)
     outgoing = pl.pallas_call(
         attend_kernel,
-        out_shape=jax.ShapeDtypeStruct((2 * nblk, wide), jnp.bfloat16),
+        out_shape=jax.ShapeDtypeStruct((mrows, wide), jnp.bfloat16),
         in_specs=[pl.BlockSpec(memory_space=pltpu.SMEM)] + [vmem] * 10,
         out_specs=vmem,
         scratch_shapes=[pltpu.VMEM(queries.shape, jnp.float32)],
@@ -210,15 +399,7 @@
         out_weight,
         route,
     )
-    arrived = lax.all_to_all(
-        outgoing.reshape(nblk, 2, wide), "blk", split_axis=0, concat_axis=0, tiled=True
-    )
-    return pl.pallas_call(
-        place_kernel,
-        out_shape=jax.ShapeDtypeStruct((capacity, 4 * width), jnp.bfloat16),
-        in_specs=[vmem],
-        out_specs=vmem,
-    )(arrived.reshape(2 * nblk, wide))
+    return route_rows(outgoing, nblk, capacity)
 
 
 def solution(mesh):

time: 229 us -> 186 us (0.81)
  blocking collectives: 145 us -> 0 us
  Pallas kernels: 62.1 us -> 174 us
  local copies, waits for them, and re-layouts: 20.7 us -> 10 us
    all_to_all x1 -> x0, blocking collectives: 145 us -> none  [per_device(): lax.all_to_all(outgoing.reshape(nblk, 2, wide), 'blk', split_axis=0, conc...]
    pallas_call x2, Pallas kernels: 14.6 us -> 127 us  [the longest x1 117 us: route_rows(): pl.pallas_call(functools.partial(route_kernel, nblk), out_shape=jax.Shape...]
    reshape x2 -> x0, local copies, waits for them, and re-layouts: 11.8 us -> none  [the longest x1 6.57 us: per_device(): arrived.reshape(2 * nblk, wide)]
    unnamed x14 -> x15, local copies, waits for them, and re-layouts: 7.81 us -> 8.87 us
where the time goes in v2:
time: 186 us; the launch traced here: 185 us
  Pallas kernels  174 us (94%)
  local copies, waits for them, and re-layouts  10 us (5%)
    pallas_call x1, Pallas kernels, route_rows(): pl.pallas_call(functools.partial(route_kernel, nblk), out_shape=jax.Shape...  117 us
    pallas_call x1, Pallas kernels, halo(): pl.pallas_call(functools.partial(halo_kernel, nblk), out_shape=(shape, sh...  47.5 us
    pallas_call x1, Pallas kernels, per_device(): pl.pallas_call(attend_kernel, out_shape=jax.ShapeDtypeStruct((mrows, wide...  9.52 us
    unnamed x15, local copies, waits for them, and re-layouts  8.87 us

profile of v2, /device:TPU:24, one launch (start us, length us, event | category | flops | bytes accessed | tf_op | source)
XLA Modules:
  0.0 184.7 jit_solution(9788198078287633727)
XLA Ops:
  0.0 0.7 pad_add_fusion
  0.7 0.1 broadcast_in_dim.2
  0.8 0.1 reshape.12.route_ref
  0.9 0.9 reshape.11.seg_ref
  1.8 47.5 %shard_map.91 = (bf16[6,256,640]{2,1,0:T(8,128)(2,1)}, bf16[6,256,640]{2,1,0:T(8,128)(2,1)}) custom-call(bf16[256,640]{1,0:T(8,128)(2,1)} %k_ref.3, bf16[256,640]{1,0:T(8,128)(2,1)} %v_ref.3), custom_call_target="tpu_custom_call" | custom-call | tf_op jit(solution)/shard_map/pallas_call | solution.py:80
  49.3 0.0 copy-start
  49.3 1.5 copy-done
  50.8 0.0 copy-start.1
  50.9 1.4 copy-done.1
  52.3 0.0 copy-start.2
  52.3 1.0 copy-done.2
  53.3 0.0 copy-start.3
  53.3 1.0 copy-done.3
  54.2 0.0 copy-start.4
  54.2 1.1 copy-done.4
  55.3 0.0 copy-start.5
  55.3 1.0 copy-done.5
  56.3 0.0 copy-start.6
  56.3 0.8 copy-done.6
  57.1 9.5 %shard_map.92.r_ref = bf16[64,5248]{1,0:T(8,128)(2,1)S(1)} custom-call(s32[1]{0:T(128)} %bitcast.here, bf16[256,640]{1,0:T(8,128)(2,1)S(1)} %copy-done.5, bf16[256,640]{1,0:T(8,128)(2,1)S(1)} %copy-done.2, bf16[256,640]{1,0:T(8,128)(2,1)S(1)} %copy-done.3, bf16[6,256,640]{2,1,0:T(8,128)(2,1)S(1)} %copy-done, bf16[6,256,640]{2,1,0:T(8,128)(2,1)} %get-tuple-element.8.vh, ...), custom_call_target="tpu_custom_call" | custom-call | tf_op jit(solution)/shard_map/pallas_call | solution.py:382
  66.7 117.0 %shard_map.93 = bf16[128,5120]{1,0:T(8,128)(2,1)S(1)} custom-call(bf16[64,5248]{1,0:T(8,128)(2,1)S(1)} %shard_map.92.r_ref), custom_call_target="tpu_custom_call" | custom-call | tf_op jit(solution)/shard_map/pallas_call | solution.py:351
  183.7 1.1 copy.11
Async XLA Ops:
  49.3 1.5 copy-start
  50.8 1.4 copy-start.1
  52.3 1.0 copy-start.2
  53.3 1.0 copy-start.3
  54.2 1.1 copy-start.4
  55.3 1.0 copy-start.5
  56.3 0.8 copy-start.6

commit v3 on v2

--- a/solution.py
+++ b/solution.py
@@ -14,77 +14,7 @@
 PLANE = 8
 REACH = 4
 CHUNKS = 4
-
-
-def halo_kernel(nblk, k_ref, v_ref, kh, vh, ksend, vsend, krecv, vrecv):
-    me = lax.axis_index("blk")
-    rungs = nblk // 2
-    rung, side = lax.div(me, 2), lax.rem(me, 2)
-    up = lax.rem(rung + 1, rungs) * 2 + side
-    down = lax.rem(rung + rungs - 1, rungs) * 2 + side
-    across = rung * 2 + 1 - side
-    far = lax.rem(rung + 1 - 2 * side + rungs, rungs) * 2 + side
-
-    barrier = pltpu.get_barrier_semaphore()
-    for other in (up, down, across):
-        pl.semaphore_signal(barrier, inc=1, device_id={"blk": other}, device_id_type=pl.DeviceIdType.MESH)
-    pl.semaphore_wait(barrier, 3)
-
-    def send(src, dst, sends, recvs, number, slot, target):
-        copy = pltpu.make_async_remote_copy(
-            src_ref=src,
-            dst_ref=dst.at[slot],
-            send_sem=sends.at[number],
-            recv_sem=recvs.at[slot],
-            device_id={"blk": target},
-            device_id_type=pl.DeviceIdType.MESH,
-        )
-        copy.start()
-        return copy
-
-    def arrived(dst, recvs, slot):
-        pltpu.make_async_copy(dst.at[slot], dst.at[slot], recvs.at[slot]).wait()
-
-    started = []
-    started.append(send(v_ref, vh, vsend, vrecv, 0, 2 + side, across))
-    started.append(send(k_ref, kh, ksend, krecv, 1, 1, up))
-    started.append(send(k_ref, kh, ksend, krecv, 2, 4, down))
-    started.append(send(k_ref, kh, ksend, krecv, 0, 2 + side, across))
-    started.append(send(v_ref, vh, vsend, vrecv, 1, 1, up))
-    started.append(send(v_ref, vh, vsend, vrecv, 2, 4, down))
-    arrived(vh, vrecv, 3 - side)
-    started.append(send(vh.at[3 - side], vh, vsend, vrecv, 3, 2 - 2 * side, up))
-    started.append(send(vh.at[3 - side], vh, vsend, vrecv, 4, 5 - 2 * side, down))
-    arrived(kh, krecv, 1)
-    started.append(send(kh.at[1], kh, ksend, krecv, 3, 2 * side, across))
-    arrived(kh, krecv, 4)
-    started.append(send(kh.at[4], kh, ksend, krecv, 4, 3 + 2 * side, across))
-    arrived(kh, krecv, 2 - 2 * side)
-    arrived(kh, krecv, 5 - 2 * side)
-    started.append(send(kh.at[2 + side], kh, ksend, krecv, 5, 5 * side, far))
-    arrived(vh, vrecv, 2 - 2 * side)
-    arrived(vh, vrecv, 5 - 2 * side)
-    started.append(send(vh.at[2 + side], vh, vsend, vrecv, 5, 5 * side, far))
-    arrived(kh, krecv, 3 - side)
-    arrived(vh, vrecv, 1)
-    arrived(vh, vrecv, 4)
-    arrived(kh, krecv, 5 * side)
-    arrived(vh, vrecv, 5 * side)
-    for copy in started:
-        copy.wait_send()
-
-
-def halo(keys, values, nblk):
-    rows, features = keys.shape
-    shape = jax.ShapeDtypeStruct((2 * SPAN, rows, features), keys.dtype)
-    return pl.pallas_call(
-        functools.partial(halo_kernel, nblk),
-        out_shape=(shape, shape),
-        in_specs=[pl.BlockSpec(memory_space=pl.ANY)] * 2,
-        out_specs=(pl.BlockSpec(memory_space=pl.ANY),) * 2,
-        scratch_shapes=[pltpu.SemaphoreType.DMA((6,))] * 4,
-        compiler_params=pltpu.CompilerParams(collective_id=0, has_side_effects=True),
-    )(keys, values)
+PARTS = 2
 
 
 def to_column(row):
@@ -96,55 +26,175 @@
 
 
 def attend_kernel(
-    here, q_ref, k_ref, v_ref, kh, vh, seg_ref, mask_ref, tok_ref, w_ref, route_ref, out_ref, att
+    q_hbm, k_hbm, v_hbm, seg_hbm, mask_hbm, tok_hbm, w_hbm, route_hbm, out_ref,
+    q_ref, k_ref, v_ref, seg_ref, mask_ref, tok_ref, w_ref, route_ref,
+    kh, vh, peaks, totals, mixed, loads, ksend, vsend, krecv, vrecv,
 ):
     rows, features = q_ref.shape
     nblk = seg_ref.shape[0]
     width = tok_ref.shape[1]
     hdim = features // HEADS
-    block = here[0]
+    block = lax.axis_index("blk")
     scale = 1.0 / jnp.sqrt(jnp.float32(hdim))
+
+    pairs = [
+        (q_hbm, q_ref),
+        (k_hbm, k_ref),
+        (v_hbm, v_ref),
+        (seg_hbm, seg_ref),
+        (mask_hbm, mask_ref),
+        (route_hbm, route_ref),
+        (tok_hbm, tok_ref),
+        (w_hbm, w_ref),
+    ]
+    local = [pltpu.make_async_copy(src, dst, loads.at[n]) for n, (src, dst) in enumerate(pairs)]
+    for copy in local:
+        copy.start()
+
+    rungs = nblk // 2
+    rung, side = lax.div(block, 2), lax.rem(block, 2)
+    up = lax.rem(rung + 1, rungs) * 2 + side
+    down = lax.rem(rung + rungs - 1, rungs) * 2 + side
+    across = rung * 2 + 1 - side
+    far = lax.rem(rung + 1 - 2 * side + rungs, rungs) * 2 + side
+    back = lax.rem(rung - 1 + 2 * side + rungs, rungs) * 2 + side
+
+    barrier = pltpu.get_barrier_semaphore()
+    for other in (up, down, across):
+        pl.semaphore_signal(barrier, inc=1, device_id={"blk": other}, device_id_type=pl.DeviceIdType.MESH)
+    pl.semaphore_wait(barrier, 3)
+
+    half = rows // PARTS
+    started = []
+
+    def send(src, dst, sends, recvs, number, slot, part, target):
+        span = pl.ds(part * half, half)
+        copy = pltpu.make_async_remote_copy(
+            src_ref=src.at[span],
+            dst_ref=dst.at[slot, span],
+            send_sem=sends.at[number * PARTS + part],
+            recv_sem=recvs.at[slot * PARTS + part],
+            device_id={"blk": target},
+            device_id_type=pl.DeviceIdType.MESH,
+        )
+        copy.start()
+        started.append(copy)
+
+    def arrived(dst, recvs, slot, part):
+        span = pl.ds(part * half, half)
+        pltpu.make_async_copy(
+            dst.at[slot, span], dst.at[slot, span], recvs.at[slot * PARTS + part]
+        ).wait()
+
+    for part in range(PARTS):
+        send(v_hbm, vh, vsend, vrecv, 0, 2 + side, part, across)
+        send(k_hbm, kh, ksend, krecv, 1, 4 - 3 * side, part, back)
+        send(k_hbm, kh, ksend, krecv, 2, 1 + 3 * side, part, far)
+    for part in range(PARTS):
+        send(k_hbm, kh, ksend, krecv, 0, 2 + side, part, across)
+        send(v_hbm, vh, vsend, vrecv, 2, 1 + 3 * side, part, far)
+        send(v_hbm, vh, vsend, vrecv, 1, 4 - 3 * side, part, back)
+    for part in range(PARTS):
+        arrived(vh, vrecv, 3 - side, part)
+        send(vh.at[3 - side], vh, vsend, vrecv, 3, 2 + side, part, far)
+        send(vh.at[3 - side], vh, vsend, vrecv, 4, 5 - 5 * side, part, back)
+    for part in range(PARTS):
+        arrived(kh, krecv, 4 - 3 * side, part)
+        send(kh.at[4 - 3 * side], kh, ksend, krecv, 3, 3 - side, part, across)
+    for part in range(PARTS):
+        arrived(kh, krecv, 1 + 3 * side, part)
+        send(kh.at[1 + 3 * side], kh, ksend, krecv, 4, 5 * side, part, across)
+
+    for copy in local:
+        copy.wait()
     query_seg = to_column(seg_ref[pl.ds(block, 1), :])
     mask_row = mask_ref[pl.ds(block, 1), :]
     columns = lax.broadcasted_iota(jnp.int32, mask_row.shape, 1)
-    key_segs, sources = [], []
-    for dist in range(-SPAN, SPAN + 1):
+
+    def segments(dist):
         column = block + dist
         flag = jnp.sum(jnp.where(columns == column, mask_row, 0), axis=1, keepdims=True)
-        ids = seg_ref[pl.ds(jnp.clip(column, 0, nblk - 1), 1), :]
-        key_segs.append(jnp.where(flag > 0, ids, -1))
-        if dist == 0:
-            sources.append((k_ref, v_ref))
-        else:
-            slot = dist + SPAN - (1 if dist > 0 else 0)
-            sources.append((kh.at[slot], vh.at[slot]))
-    for head in range(HEADS):
+        ids = seg_ref[pl.ds(lax.rem(column + nblk, nblk), 1), :]
+        return jnp.where(flag > 0, ids, -1)
+
+    def window(head):
         first, last = head * hdim, (head + 1) * hdim
-        low = first // LANES * LANES
-        high = -(-last // LANES) * LANES
+        low, high = first // LANES * LANES, -(-last // LANES) * LANES
         lane = lax.broadcasted_iota(jnp.int32, (rows, high - low), 1) + low
-        mine = (lane >= first) & (lane < last)
-        query = jnp.where(mine, q_ref[:, low:high], jnp.bfloat16(0))
-        scores = []
-        for (key, _), key_seg in zip(sources, key_segs):
-            part = lax.dot_general(
-                query, key[:, low:high], (((1,), (1,)), ((), ())), preferred_element_type=jnp.float32
-            )
-            scores.append(jnp.where(query_seg == key_seg, part, NEG))
-        peak = functools.reduce(jnp.maximum, scores)
-        peak = jnp.max(peak, axis=1, keepdims=True)
-        total = jnp.zeros((rows, 1), jnp.float32)
-        mixed = jnp.zeros((rows, high - low), jnp.float32)
-        for (_, value), part in zip(sources, scores):
-            weights = jnp.exp((part - peak) * scale)
-            total = total + jnp.sum(weights, axis=1, keepdims=True)
-            mixed = mixed + jnp.dot(
-                weights.astype(jnp.bfloat16), value[:, low:high], preferred_element_type=jnp.float32
-            )
-        att[:, low:high] = jnp.where(mine, mixed / total, att[:, low:high])
+        return low, high, (lane >= first) & (lane < last)
+
+    def attend(blocks, fresh):
+        for head in range(HEADS):
+            low, high, mine = window(head)
+            query = jnp.where(mine, q_ref[:, low:high], jnp.bfloat16(0))
+            scores = []
+            for key, _, key_seg in blocks:
+                part = lax.dot_general(
+                    query,
+                    key[:, low:high],
+                    (((1,), (1,)), ((), ())),
+                    preferred_element_type=jnp.float32,
+                )
+                scores.append(jnp.where(query_seg == key_seg, part, NEG))
+            peak = jnp.max(functools.reduce(jnp.maximum, scores), axis=1, keepdims=True)
+            if fresh:
+                total = jnp.zeros((rows, 1), jnp.float32)
+                result = jnp.zeros((rows, high - low), jnp.float32)
+            else:
+                before = peaks[head]
+                peak = jnp.maximum(peak, before)
+                factor = jnp.exp((before - peak) * scale)
+                total = totals[head] * factor
+                result = mixed[head, :, : high - low] * factor
+            for (_, value, _), part in zip(blocks, scores):
+                weights = jnp.exp((part - peak) * scale)
+                total = total + jnp.sum(weights, axis=1, keepdims=True)
+                result = result + jnp.dot(
+                    weights.astype(jnp.bfloat16), value[:, low:high], preferred_element_type=jnp.float32
+                )
+            peaks[head] = peak
+            totals[head] = total
+            mixed[head, :, : high - low] = result
+
+    def held(slot, dist):
+        return kh.at[slot], vh.at[slot], segments(dist)
+
+    for part in range(PARTS):
+        arrived(kh, krecv, 3 - side, part)
+        arrived(vh, vrecv, 1, part)
+        arrived(vh, vrecv, 4, part)
+    attend(
+        [(k_ref, v_ref, segments(0)), held(3 - side, 1 - 2 * side), held(1, -2), held(4, 2)], True
+    )
+    for part in range(PARTS):
+        arrived(vh, vrecv, 2 + side, part)
+        send(vh.at[2 + side], vh, vsend, vrecv, 5, 5 * side, part, far)
+    for part in range(PARTS):
+        arrived(kh, krecv, 2 + side, part)
+        send(kh.at[2 + side], kh, ksend, krecv, 5, 5 * side, part, far)
+    for part in range(PARTS):
+        arrived(vh, vrecv, 5 - 5 * side, part)
+        arrived(kh, krecv, 5 - 5 * side, part)
+    attend([held(2 + side, 2 * side - 1), held(5 - 5 * side, 3 - 6 * side)], False)
+    for part in range(PARTS):
+        arrived(vh, vrecv, 5 * side, part)
+        arrived(kh, krecv, 5 * side, part)
+    attend([held(5 * side, 6 * side - 3)], False)
+
+    pieces = []
+    for group in range(features // LANES):
+        piece = jnp.zeros((rows, LANES), jnp.float32)
+        for head in range(HEADS):
+            low, high, mine = window(head)
+            start = group * LANES - low
+            if 0 <= start < high - low:
+                ready = mixed[head, :, start : start + LANES] / totals[head]
+                piece = jnp.where(mine[:, start : start + LANES], ready, piece)
+        pieces.append(piece.astype(jnp.bfloat16))
+    attended = jnp.concatenate(pieces, axis=1)
     hidden = (
         tok_ref[...].astype(jnp.float32)
-        + jnp.dot(att[...].astype(jnp.bfloat16), w_ref[...], preferred_element_type=jnp.float32)
+        + jnp.dot(attended, w_ref[...], preferred_element_type=jnp.float32)
     ).astype(jnp.bfloat16)
     owner_row = route_ref[0:1, :]
     owner_col = to_column(owner_row)
@@ -168,6 +218,8 @@
         out_ref[:, start : start + width] = jnp.dot(
             pick.astype(jnp.float32).astype(jnp.bfloat16), hidden, preferred_element_type=jnp.float32
         ).astype(jnp.bfloat16)
+    for copy in started:
+        copy.wait_send()
 
 
 def to_row(column):
@@ -198,8 +250,10 @@
     plane, spot = lax.div(me, PLANE), lax.rem(me, PLANE)
     mrows, wide = r_ref.shape
     per = 2 * PLANE
-    step = (wide - LANES) // CHUNKS
-    chunks = [(0, LANES + step)] + [(LANES + c * step, step) for c in range(1, CHUNKS)]
+    unit = (wide - LANES) // 20
+    chunks = [(0, LANES + 5 * unit)]
+    for share in (6, 6, 3):
+        chunks.append((sum(chunks[-1]), share * unit))
 
     def along(distance):
         return lax.rem(plane + distance + planes, planes) * PLANE + spot
@@ -375,30 +429,38 @@
     mrows = rows // 4
     capacity = 2 * mrows
     wide = 4 * width + LANES
-    key_halo, value_halo = halo(keys, values, nblk)
-    here = lax.axis_index("blk").reshape(1)
     route = jnp.broadcast_to(jnp.stack([owners, offsets])[:, :, None], (2, mrows, 4)).reshape(2, rows)
-    vmem = pl.BlockSpec(memory_space=pltpu.VMEM)
-    outgoing = pl.pallas_call(
-        attend_kernel,
-        out_shape=jax.ShapeDtypeStruct((mrows, wide), jnp.bfloat16),
-        in_specs=[pl.BlockSpec(memory_space=pltpu.SMEM)] + [vmem] * 10,
-        out_specs=vmem,
-        scratch_shapes=[pltpu.VMEM(queries.shape, jnp.float32)],
-        compiler_params=pltpu.CompilerParams(vmem_limit_bytes=48 * 2**20),
-    )(
-        here,
+    operands = (
         queries,
         keys,
         values,
-        key_halo,
-        value_halo,
         segment_ids.reshape(nblk, rows),
         block_mask,
         tokens,
         out_weight,
         route,
     )
+    halo = pltpu.VMEM((2 * SPAN,) + keys.shape, keys.dtype)
+    dma = pltpu.SemaphoreType.DMA
+    outgoing = pl.pallas_call(
+        attend_kernel,
+        out_shape=jax.ShapeDtypeStruct((mrows, wide), jnp.bfloat16),
+        in_specs=[pl.BlockSpec(memory_space=pl.ANY)] * len(operands),
+        out_specs=pl.BlockSpec(memory_space=pltpu.VMEM),
+        scratch_shapes=[pltpu.VMEM(x.shape, x.dtype) for x in operands]
+        + [
+            halo,
+            halo,
+            pltpu.VMEM((HEADS, rows, 1), jnp.float32),
+            pltpu.VMEM((HEADS, rows, 1), jnp.float32),
+            pltpu.VMEM((HEADS, rows, 2 * LANES), jnp.float32),
+            dma((len(operands),)),
+        ]
+        + [dma((2 * SPAN * PARTS,))] * 4,
+        compiler_params=pltpu.CompilerParams(
+            collective_id=0, has_side_effects=True, vmem_limit_bytes=56 * 2**20
+        ),
+    )(*operands)
     return route_rows(outgoing, nblk, capacity)
 
 

time: 186 us -> 173 us (0.930)
  Pallas kernels: 174 us -> 165 us
  local copies, waits for them, and re-layouts: 10 us -> 4.5 us
    pallas_call x1 -> x0, Pallas kernels: 47.5 us -> none  [halo(): pl.pallas_call(functools.partial(halo_kernel, nblk), out_shape=(shape, sh...]
    pallas_call x1, Pallas kernels: 9.52 us -> 44.7 us  [per_device(): pl.pallas_call(attend_kernel, out_shape=jax.ShapeDtypeStruct((mrows, wide...]
    unnamed x15 -> x3, local copies, waits for them, and re-layouts: 8.87 us -> 2.15 us
    pallas_call x1, Pallas kernels: 117 us -> 121 us  [route_rows(): pl.pallas_call(functools.partial(route_kernel, nblk), out_shape=jax.Shape...]
where the time goes in v3:
time: 173 us; the launch traced here: 171 us
  Pallas kernels  165 us (95%)
  local copies, waits for them, and re-layouts  4.5 us (3%)
    pallas_call x1, Pallas kernels, route_rows(): pl.pallas_call(functools.partial(route_kernel, nblk), out_shape=jax.Shape...  121 us
    pallas_call x1, Pallas kernels, per_device(): pl.pallas_call(attend_kernel, out_shape=jax.ShapeDtypeStruct((mrows, wide...  44.7 us

profile of v3, /device:TPU:24, one launch (start us, length us, event | category | flops | bytes accessed | tf_op | source)
XLA Modules:
  0.0 170.6 jit_solution(1487672790614069142)
XLA Ops:
  0.0 0.7 pad_add_fusion
  0.7 0.1 broadcast_in_dim.2
  0.8 0.7 reshape.8.route_hbm
  1.4 1.6 reshape.7.seg_hbm
  3.0 44.7 %shard_map.91.r_ref = bf16[64,5248]{1,0:T(8,128)(2,1)} custom-call(bf16[256,640]{1,0:T(8,128)(2,1)} %q_hbm.1, bf16[256,640]{1,0:T(8,128)(2,1)} %k_hbm.1, bf16[256,640]{1,0:T(8,128)(2,1)} %v_hbm.1, s32[128,256]{1,0:T(8,128)} %reshape.7.seg_hbm, s32[128,128]{1,0:T(8,128)} %mask_hbm.1, bf16[256,1280]{1,0:T(8,128)(2,1)} %tok_hbm.1, bf16[640,1280]{1,0:T(8,128)(2,1)} %w_hbm.1, ...), custom_call_target="tpu_custom_call" | custom-call | tf_op jit(solution)/shard_map/pallas_call | solution.py:445
  47.8 0.0 copy-start
  47.8 1.1 copy-done
  48.9 120.7 %shard_map.92 = bf16[128,5120]{1,0:T(8,128)(2,1)S(1)} custom-call(bf16[64,5248]{1,0:T(8,128)(2,1)S(1)} %copy-done), custom_call_target="tpu_custom_call" | custom-call | tf_op jit(solution)/shard_map/pallas_call | solution.py:405
  169.5 1.1 copy.11
Async XLA Ops:
  47.8 1.1 copy-start

commit v4 on v3

--- a/solution.py
+++ b/solution.py
@@ -25,13 +25,34 @@
     return jnp.sum(jnp.where(diagonal, row, 0), axis=1, keepdims=True)
 
 
-def attend_kernel(
-    q_hbm, k_hbm, v_hbm, seg_hbm, mask_hbm, tok_hbm, w_hbm, route_hbm, out_ref,
-    q_ref, k_ref, v_ref, seg_ref, mask_ref, tok_ref, w_ref, route_ref,
-    kh, vh, peaks, totals, mixed, loads, ksend, vsend, krecv, vrecv,
+def to_row(column):
+    size = column.shape[0]
+    diagonal = lax.broadcasted_iota(jnp.int32, (size, size), 0) == lax.broadcasted_iota(
+        jnp.int32, (size, size), 1
+    )
+    return jnp.sum(jnp.where(diagonal, column, 0.0), axis=0, keepdims=True)
+
+
+def codes_of(tags):
+    return to_row(tags.astype(jnp.float32)[:, LANES // 2 : LANES // 2 + 1])
+
+
+def as_onehot(hit):
+    return jnp.where(hit, 1.0, 0.0).astype(jnp.bfloat16)
+
+
+def pick_rows(onehot, rows):
+    return jnp.dot(onehot, rows, preferred_element_type=jnp.float32)
+
+
+def program_kernel(
+    q_hbm, k_hbm, v_hbm, seg_hbm, mask_hbm, tok_hbm, w_hbm, owner_hbm, offset_hbm, out_ref,
+    q_ref, k_ref, v_ref, seg_ref, mask_ref, tok_ref, w_ref, owner_ref, offset_ref,
+    kh, vh, peaks, totals, mixed, r_ref, near, comp, far_rows, ordered, landed,
+    loads, ksend, vsend, krecv, vrecv, nsend, nrecv, fsend, frecv, psend, precv,
 ):
     rows, features = q_ref.shape
-    nblk = seg_ref.shape[0]
+    nblk = mask_ref.shape[0]
     width = tok_ref.shape[1]
     hdim = features // HEADS
     block = lax.axis_index("blk")
@@ -43,7 +64,8 @@
         (v_hbm, v_ref),
         (seg_hbm, seg_ref),
         (mask_hbm, mask_ref),
-        (route_hbm, route_ref),
+        (owner_hbm, owner_ref),
+        (offset_hbm, offset_ref),
         (tok_hbm, tok_ref),
         (w_hbm, w_ref),
     ]
@@ -59,10 +81,22 @@
     far = lax.rem(rung + 1 - 2 * side + rungs, rungs) * 2 + side
     back = lax.rem(rung - 1 + 2 * side + rungs, rungs) * 2 + side
 
+    planes = nblk // PLANE
+    plane, spot = lax.div(block, PLANE), lax.rem(block, PLANE)
+
+    def along(distance):
+        return lax.rem(plane + distance + planes, planes) * PLANE + spot
+
+    def within(distance):
+        return plane * PLANE + lax.rem(spot + distance, PLANE)
+
     barrier = pltpu.get_barrier_semaphore()
-    for other in (up, down, across):
+    peers = [up, down, across]
+    peers += [along(d) for k in range(1, REACH + 1) for d in (k, -k)]
+    peers += [within(d) for d in range(1, PLANE)]
+    for other in peers:
         pl.semaphore_signal(barrier, inc=1, device_id={"blk": other}, device_id_type=pl.DeviceIdType.MESH)
-    pl.semaphore_wait(barrier, 3)
+    pl.semaphore_wait(barrier, len(peers))
 
     half = rows // PARTS
     started = []
@@ -107,15 +141,21 @@
 
     for copy in local:
         copy.wait()
-    query_seg = to_column(seg_ref[pl.ds(block, 1), :])
+
+    def ids_of(column):
+        halves = rows // LANES
+        return jnp.concatenate(
+            [seg_ref[pl.ds(column * halves + n, 1), :] for n in range(halves)], axis=1
+        )
+
+    query_seg = to_column(ids_of(block))
     mask_row = mask_ref[pl.ds(block, 1), :]
     columns = lax.broadcasted_iota(jnp.int32, mask_row.shape, 1)
 
     def segments(dist):
         column = block + dist
         flag = jnp.sum(jnp.where(columns == column, mask_row, 0), axis=1, keepdims=True)
-        ids = seg_ref[pl.ds(lax.rem(column + nblk, nblk), 1), :]
-        return jnp.where(flag > 0, ids, -1)
+        return jnp.where(flag > 0, ids_of(lax.rem(column + nblk, nblk)), -1)
 
     def window(head):
         first, last = head * hdim, (head + 1) * hdim
@@ -176,6 +216,17 @@
         arrived(vh, vrecv, 5 - 5 * side, part)
         arrived(kh, krecv, 5 - 5 * side, part)
     attend([held(2 + side, 2 * side - 1), held(5 - 5 * side, 3 - 6 * side)], False)
+    owner_row = owner_ref[...]
+    mrows, wide = r_ref.shape
+    earlier = (to_column(owner_row) == owner_row) & (
+        lax.broadcasted_iota(jnp.int32, (mrows, mrows), 0)
+        < lax.broadcasted_iota(jnp.int32, (mrows, mrows), 1)
+    )
+    rank = jnp.sum(earlier.astype(jnp.int32), axis=0, keepdims=True)
+    lane = lax.broadcasted_iota(jnp.int32, (mrows, LANES), 1)
+    offset, code = to_column(offset_ref[...]), to_column(2 * owner_row + rank)
+    tags = jnp.where(lane < LANES // 2, offset + 1, code + 1)
+    r_ref[:, :LANES] = tags.astype(jnp.float32).astype(jnp.bfloat16)
     for part in range(PARTS):
         arrived(vh, vrecv, 5 * side, part)
         arrived(kh, krecv, 5 * side, part)
@@ -196,81 +247,15 @@
         tok_ref[...].astype(jnp.float32)
         + jnp.dot(attended, w_ref[...], preferred_element_type=jnp.float32)
     ).astype(jnp.bfloat16)
-    owner_row = route_ref[0:1, :]
-    owner_col = to_column(owner_row)
-    down = lax.broadcasted_iota(jnp.int32, (rows, rows), 0)
-    right = lax.broadcasted_iota(jnp.int32, (rows, rows), 1)
-    earlier = (owner_col == owner_row) & (down < right // 4 * 4) & (down % 4 == 0)
-    rank = jnp.sum(earlier.astype(jnp.int32), axis=0, keepdims=True)
-    slot = 2 * owner_row + rank
-    mrows = rows // 4
     merged = lax.broadcasted_iota(jnp.int32, (mrows, rows), 0)
     source = lax.broadcasted_iota(jnp.int32, (mrows, rows), 1)
-    lane = lax.broadcasted_iota(jnp.int32, (mrows, LANES), 1)
-    for quarter in range(4):
-        pick = source == 4 * merged + quarter
-        if quarter == 0:
-            offset = jnp.sum(jnp.where(pick, route_ref[1:2, :], 0), axis=1, keepdims=True)
-            code = jnp.sum(jnp.where(pick, slot, 0), axis=1, keepdims=True)
-            tags = jnp.where(lane < LANES // 2, offset + 1, code + 1)
-            out_ref[:, :LANES] = tags.astype(jnp.float32).astype(jnp.bfloat16)
-        start = LANES + quarter * width
-        out_ref[:, start : start + width] = jnp.dot(
-            pick.astype(jnp.float32).astype(jnp.bfloat16), hidden, preferred_element_type=jnp.float32
-        ).astype(jnp.bfloat16)
-    for copy in started:
-        copy.wait_send()
-
-
-def to_row(column):
-    size = column.shape[0]
-    diagonal = lax.broadcasted_iota(jnp.int32, (size, size), 0) == lax.broadcasted_iota(
-        jnp.int32, (size, size), 1
-    )
-    return jnp.sum(jnp.where(diagonal, column, 0.0), axis=0, keepdims=True)
-
-
-def codes_of(tags):
-    return to_row(tags.astype(jnp.float32)[:, LANES // 2 : LANES // 2 + 1])
-
-
-def as_onehot(hit):
-    return jnp.where(hit, 1.0, 0.0).astype(jnp.bfloat16)
-
-
-def pick_rows(onehot, rows):
-    return jnp.dot(onehot, rows, preferred_element_type=jnp.float32)
-
-
-def route_kernel(
-    nblk, r_ref, out_ref, near, comp, far, ordered, landed, nsend, nrecv, fsend, frecv, psend, precv
-):
-    me = lax.axis_index("blk")
-    planes = nblk // PLANE
-    plane, spot = lax.div(me, PLANE), lax.rem(me, PLANE)
-    mrows, wide = r_ref.shape
     per = 2 * PLANE
     unit = (wide - LANES) // 20
     chunks = [(0, LANES + 5 * unit)]
     for share in (6, 6, 3):
         chunks.append((sum(chunks[-1]), share * unit))
 
-    def along(distance):
-        return lax.rem(plane + distance + planes, planes) * PLANE + spot
-
-    def within(distance):
-        return plane * PLANE + lax.rem(spot + distance, PLANE)
-
-    barrier = pltpu.get_barrier_semaphore()
-    peers = [along(d) for k in range(1, REACH + 1) for d in (k, -k)]
-    peers += [within(d) for d in range(1, PLANE)]
-    for other in peers:
-        pl.semaphore_signal(barrier, inc=1, device_id={"blk": other}, device_id_type=pl.DeviceIdType.MESH)
-    pl.semaphore_wait(barrier, len(peers))
-
-    started = []
-
-    def send(src, dst, sends, recvs, number, target):
+    def pass_on(src, dst, sends, recvs, number, target):
         copy = pltpu.make_async_remote_copy(
             src_ref=src,
             dst_ref=dst,
@@ -290,7 +275,7 @@
         begin, size = chunks[chunk]
         cols = pl.ds(begin, size)
         src = r_ref.at[:, cols] if hop == 1 else near.at[pl.ds(near_at(way, hop - 1), mrows), cols]
-        return send(
+        return pass_on(
             src,
             near.at[pl.ds(near_at(way, hop), mrows), cols],
             nsend,
@@ -300,9 +285,15 @@
         )
 
     hops = {}
-    for chunk in range(CHUNKS):
-        for way in range(2):
-            hops[way, 1, chunk] = forward(way, 1, chunk)
+    built = 0
+    for quarter in range(4):
+        pick = source == 4 * merged + quarter
+        built = LANES + (quarter + 1) * width
+        r_ref[:, built - width : built] = pick_rows(as_onehot(pick), hidden).astype(jnp.bfloat16)
+        for chunk, (begin, size) in enumerate(chunks):
+            if built - width < begin + size <= built:
+                for way in range(2):
+                    hops[way, 1, chunk] = forward(way, 1, chunk)
     for hop in range(1, REACH):
         for chunk in range(CHUNKS):
             for way in range(2):
@@ -331,9 +322,9 @@
             for ahead in range(REACH, 0, -1):
                 if ahead == REACH and chunk * 2 // CHUNKS != way:
                     continue
-                relays[way, ahead, chunk] = send(
+                relays[way, ahead, chunk] = pass_on(
                     comp.at[pl.ds((way * REACH + ahead - 1) * per, per), pl.ds(begin, size)],
-                    far.at[pl.ds(far_at(way, ahead), per), pl.ds(begin, size)],
+                    far_rows.at[pl.ds(far_at(way, ahead), per), pl.ds(begin, size)],
                     fsend,
                     frecv,
                     (way * REACH + ahead - 1) * CHUNKS + chunk,
@@ -357,7 +348,7 @@
     near_hot = as_onehot(
         (group == 1 + column // mrows) & (code == (local + base).astype(jnp.float32))
     )
-    group, local, column = wanted(far.shape[0])
+    group, local, column = wanted(far_rows.shape[0])
     far_hot = as_onehot((group == 1 + 2 * REACH + column // per) & (local == column % per))
 
     spread = {}
@@ -369,10 +360,10 @@
             for ahead in range(1, REACH + 1):
                 if (way, ahead, chunk) in relays:
                     relays[way, ahead, chunk].wait_recv()
-        ordered[:, cols] = (found + pick_rows(far_hot, far[:, cols])).astype(jnp.bfloat16)
+        ordered[:, cols] = (found + pick_rows(far_hot, far_rows[:, cols])).astype(jnp.bfloat16)
         for distance in range(1, PLANE):
             theirs = pl.ds(pl.multiple_of(lax.rem(spot + distance, PLANE) * each, each), each)
-            spread[distance, chunk] = send(
+            spread[distance, chunk] = pass_on(
                 ordered.at[theirs, pl.ds(begin, size)],
                 landed.at[mine, pl.ds(begin, size)],
                 psend,
@@ -397,31 +388,6 @@
         copy.wait_send()
 
 
-def route_rows(rows, nblk, capacity):
-    mrows, wide = rows.shape
-    per = 2 * PLANE
-    vmem = pl.BlockSpec(memory_space=pltpu.VMEM)
-    dma = pltpu.SemaphoreType.DMA
-    return pl.pallas_call(
-        functools.partial(route_kernel, nblk),
-        out_shape=jax.ShapeDtypeStruct((capacity, wide - LANES), rows.dtype),
-        in_specs=[vmem],
-        out_specs=vmem,
-        scratch_shapes=[
-            pltpu.VMEM((2 * REACH * mrows, wide), rows.dtype),
-            pltpu.VMEM((2 * REACH * per, wide), rows.dtype),
-            pltpu.VMEM(((2 * REACH - 1) * per, wide), rows.dtype),
-            pltpu.VMEM((2 * nblk, wide), rows.dtype),
-            pltpu.VMEM((2 * nblk, wide), rows.dtype),
-        ]
-        + [dma((2 * REACH * CHUNKS,))] * 4
-        + [dma(((PLANE - 1) * CHUNKS,))] * 2,
-        compiler_params=pltpu.CompilerParams(
-            collective_id=1, has_side_effects=True, vmem_limit_bytes=48 * 2**20
-        ),
-    )(rows)
-
-
 def per_device(segment_ids, block_mask, queries, keys, values, tokens, out_weight, owners, offsets):
     rows = queries.shape[0]
     width = tokens.shape[1]
@@ -429,22 +395,27 @@
     mrows = rows // 4
     capacity = 2 * mrows
     wide = 4 * width + LANES
-    route = jnp.broadcast_to(jnp.stack([owners, offsets])[:, :, None], (2, mrows, 4)).reshape(2, rows)
+    per = 2 * PLANE
     operands = (
         queries,
         keys,
         values,
-        segment_ids.reshape(nblk, rows),
+        segment_ids.reshape(-1, LANES),
         block_mask,
         tokens,
         out_weight,
-        route,
+        owners.reshape(1, mrows),
+        offsets.reshape(1, mrows),
     )
     halo = pltpu.VMEM((2 * SPAN,) + keys.shape, keys.dtype)
     dma = pltpu.SemaphoreType.DMA
-    outgoing = pl.pallas_call(
-        attend_kernel,
-        out_shape=jax.ShapeDtypeStruct((mrows, wide), jnp.bfloat16),
+
+    def held(count):
+        return pltpu.VMEM((count, wide), tokens.dtype)
+
+    return pl.pallas_call(
+        program_kernel,
+        out_shape=jax.ShapeDtypeStruct((capacity, 4 * width), tokens.dtype),
         in_specs=[pl.BlockSpec(memory_space=pl.ANY)] * len(operands),
         out_specs=pl.BlockSpec(memory_space=pltpu.VMEM),
         scratch_shapes=[pltpu.VMEM(x.shape, x.dtype) for x in operands]
@@ -454,14 +425,21 @@
             pltpu.VMEM((HEADS, rows, 1), jnp.float32),
             pltpu.VMEM((HEADS, rows, 1), jnp.float32),
             pltpu.VMEM((HEADS, rows, 2 * LANES), jnp.float32),
+            held(mrows),
+            held(2 * REACH * mrows),
+            held(2 * REACH * per),
+            held((2 * REACH - 1) * per),
+            held(2 * nblk),
+            held(2 * nblk),
             dma((len(operands),)),
         ]
-        + [dma((2 * SPAN * PARTS,))] * 4,
+        + [dma((2 * SPAN * PARTS,))] * 4
+        + [dma((2 * REACH * CHUNKS,))] * 4
+        + [dma(((PLANE - 1) * CHUNKS,))] * 2,
         compiler_params=pltpu.CompilerParams(
             collective_id=0, has_side_effects=True, vmem_limit_bytes=56 * 2**20
         ),
     )(*operands)
-    return route_rows(outgoing, nblk, capacity)
 
 
 def solution(mesh):

time: 173 us -> 164 us (0.948)
  Pallas kernels: 165 us -> 159 us
  local copies, waits for them, and re-layouts: 4.5 us -> 2.46 us
    pallas_call x2 -> x1, Pallas kernels: 165 us -> 159 us  [per_device(): pl.pallas_call(program_kernel, out_shape=jax.ShapeDtypeStruct((capacity,...]
    reshape x2 -> x0, local copies, waits for them, and re-layouts: 2.28 us -> none  [the longest x1 1.6 us: per_device(): segment_ids.reshape(nblk, rows)]
where the time goes in v4:
time: 164 us; the launch traced here: 162 us
  Pallas kernels  159 us (97%)
  local copies, waits for them, and re-layouts  2.46 us (2%)
    pallas_call x1, Pallas kernels, per_device(): pl.pallas_call(program_kernel, out_shape=jax.ShapeDtypeStruct((capacity,...  159 us

profile of v4, /device:TPU:24, one launch (start us, length us, event | category | flops | bytes accessed | tf_op | source)
XLA Modules:
  0.0 161.9 jit_solution(13282046583231273435)
XLA Ops:
  0.0 159.5 %shard_map.91 = bf16[128,5120]{1,0:T(8,128)(2,1)} custom-call(bf16[256,640]{1,0:T(8,128)(2,1)} %q_hbm.1, bf16[256,640]{1,0:T(8,128)(2,1)} %k_hbm.1, bf16[256,640]{1,0:T(8,128)(2,1)} %v_hbm.1, s32[256,128]{1,0:T(8,128)} %bitcast.3, s32[128,128]{1,0:T(8,128)} %mask_hbm.1, bf16[256,1280]{1,0:T(8,128)(2,1)} %tok_hbm.1, bf16[640,1280]{1,0:T(8,128)(2,1)} %w_hbm.1, ...), custom_call_target="tpu_custom_call" | custom-call | tf_op jit(solution)/shard_map/pallas_call | solution.py:416
  159.5 2.5 %copy.11 = bf16[128,5120]{1,0:T(8,128)(2,1)} copy(bf16[128,5120]{1,0:T(8,128)(2,1)} %shard_map.91) | data formatting | bytes 2621440

commit v5 on v4

--- a/solution.py
+++ b/solution.py
@@ -128,17 +128,6 @@
         send(k_hbm, kh, ksend, krecv, 0, 2 + side, part, across)
         send(v_hbm, vh, vsend, vrecv, 2, 1 + 3 * side, part, far)
         send(v_hbm, vh, vsend, vrecv, 1, 4 - 3 * side, part, back)
-    for part in range(PARTS):
-        arrived(vh, vrecv, 3 - side, part)
-        send(vh.at[3 - side], vh, vsend, vrecv, 3, 2 + side, part, far)
-        send(vh.at[3 - side], vh, vsend, vrecv, 4, 5 - 5 * side, part, back)
-    for part in range(PARTS):
-        arrived(kh, krecv, 4 - 3 * side, part)
-        send(kh.at[4 - 3 * side], kh, ksend, krecv, 3, 3 - side, part, across)
-    for part in range(PARTS):
-        arrived(kh, krecv, 1 + 3 * side, part)
-        send(kh.at[1 + 3 * side], kh, ksend, krecv, 4, 5 * side, part, across)
-
     for copy in local:
         copy.wait()
 
@@ -199,19 +188,31 @@
     def held(slot, dist):
         return kh.at[slot], vh.at[slot], segments(dist)
 
+    attend([(k_ref, v_ref, segments(0))], True)
+    for part in range(PARTS):
+        arrived(vh, vrecv, 3 - side, part)
+        send(vh.at[3 - side], vh, vsend, vrecv, 3, 2 + side, part, far)
+        send(vh.at[3 - side], vh, vsend, vrecv, 4, 5 - 5 * side, part, back)
+    for part in range(PARTS):
+        arrived(kh, krecv, 4 - 3 * side, part)
+        send(kh.at[4 - 3 * side], kh, ksend, krecv, 3, 3 - side, part, across)
+    for part in range(PARTS):
+        arrived(kh, krecv, 1 + 3 * side, part)
+        send(kh.at[1 + 3 * side], kh, ksend, krecv, 4, 5 * side, part, across)
+
     for part in range(PARTS):
         arrived(kh, krecv, 3 - side, part)
+    attend([held(3 - side, 1 - 2 * side)], False)
+    for part in range(PARTS):
+        arrived(vh, vrecv, 2 + side, part)
+        send(vh.at[2 + side], vh, vsend, vrecv, 5, 5 * side, part, far)
+    for part in range(PARTS):
+        arrived(kh, krecv, 2 + side, part)
+        send(kh.at[2 + side], kh, ksend, krecv, 5, 5 * side, part, far)
+    for part in range(PARTS):
         arrived(vh, vrecv, 1, part)
         arrived(vh, vrecv, 4, part)
-    attend(
-        [(k_ref, v_ref, segments(0)), held(3 - side, 1 - 2 * side), held(1, -2), held(4, 2)], True
-    )
-    for part in range(PARTS):
-        arrived(vh, vrecv, 2 + side, part)
-        send(vh.at[2 + side], vh, vsend, vrecv, 5, 5 * side, part, far)
-    for part in range(PARTS):
-        arrived(kh, krecv, 2 + side, part)
-        send(kh.at[2 + side], kh, ksend, krecv, 5, 5 * side, part, far)
+    attend([held(1, -2), held(4, 2)], False)
     for part in range(PARTS):
         arrived(vh, vrecv, 5 - 5 * side, part)
         arrived(kh, krecv, 5 - 5 * side, part)
@@ -252,7 +253,7 @@
     per = 2 * PLANE
     unit = (wide - LANES) // 20
     chunks = [(0, LANES + 5 * unit)]
-    for share in (6, 6, 3):
+    for share in (7, 6, 2):
         chunks.append((sum(chunks[-1]), share * unit))
 
     def pass_on(src, dst, sends, recvs, number, target):

time: 164 us -> 166 us (1.012)
  Pallas kernels: 159 us -> 162 us
    pallas_call x1, Pallas kernels: 159 us -> 162 us  [per_device(): pl.pallas_call(program_kernel, out_shape=jax.ShapeDtypeStruct((capacity,...]
where the time goes in v5:
time: 166 us; the launch traced here: 164 us
  Pallas kernels  162 us (98%)
  local copies, waits for them, and re-layouts  2.46 us (1%)
    pallas_call x1, Pallas kernels, per_device(): pl.pallas_call(program_kernel, out_shape=jax.ShapeDtypeStruct((capacity,...  162 us

profile of v5, /device:TPU:24, one launch (start us, length us, event | category | flops | bytes accessed | tf_op | source)
XLA Modules:
  0.0 164.5 jit_solution(6443288742708222014)
XLA Ops:
  0.0 162.0 %shard_map.91 = bf16[128,5120]{1,0:T(8,128)(2,1)} custom-call(bf16[256,640]{1,0:T(8,128)(2,1)} %q_hbm.1, bf16[256,640]{1,0:T(8,128)(2,1)} %k_hbm.1, bf16[256,640]{1,0:T(8,128)(2,1)} %v_hbm.1, s32[256,128]{1,0:T(8,128)} %bitcast.3, s32[128,128]{1,0:T(8,128)} %mask_hbm.1, bf16[256,1280]{1,0:T(8,128)(2,1)} %tok_hbm.1, bf16[640,1280]{1,0:T(8,128)(2,1)} %w_hbm.1, ...), custom_call_target="tpu_custom_call" | custom-call | tf_op jit(solution)/shard_map/pallas_call | solution.py:417
  162.0 2.5 %copy.11 = bf16[128,5120]{1,0:T(8,128)(2,1)} copy(bf16[128,5120]{1,0:T(8,128)(2,1)} %shard_map.91) | data formatting | bytes 2621440

commit v6 on v4

--- a/solution.py
+++ b/solution.py
@@ -13,7 +13,7 @@
 LANES = 128
 PLANE = 8
 REACH = 4
-CHUNKS = 4
+CHUNKS = 5
 PARTS = 2
 
 
@@ -250,10 +250,8 @@
     merged = lax.broadcasted_iota(jnp.int32, (mrows, rows), 0)
     source = lax.broadcasted_iota(jnp.int32, (mrows, rows), 1)
     per = 2 * PLANE
-    unit = (wide - LANES) // 20
-    chunks = [(0, LANES + 5 * unit)]
-    for share in (6, 6, 3):
-        chunks.append((sum(chunks[-1]), share * unit))
+    step = (wide - LANES) // CHUNKS
+    chunks = [(0, LANES + step)] + [(LANES + c * step, step) for c in range(1, CHUNKS)]
 
     def pass_on(src, dst, sends, recvs, number, target):
         copy = pltpu.make_async_remote_copy(

time: 164 us -> 161 us (0.982)
  Pallas kernels: 159 us -> 157 us
    pallas_call x1, Pallas kernels: 159 us -> 157 us  [per_device(): pl.pallas_call(program_kernel, out_shape=jax.ShapeDtypeStruct((capacity,...]
where the time goes in v6:
time: 161 us; the launch traced here: 160 us
  Pallas kernels  157 us (98%)
  local copies, waits for them, and re-layouts  2.46 us (2%)
    pallas_call x1, Pallas kernels, per_device(): pl.pallas_call(program_kernel, out_shape=jax.ShapeDtypeStruct((capacity,...  157 us

profile of v6, /device:TPU:24, one launch (start us, length us, event | category | flops | bytes accessed | tf_op | source)
XLA Modules:
  0.0 159.9 jit_solution(6511171071399460209)
XLA Ops:
  0.0 157.4 %shard_map.91 = bf16[128,5120]{1,0:T(8,128)(2,1)} custom-call(bf16[256,640]{1,0:T(8,128)(2,1)} %q_hbm.1, bf16[256,640]{1,0:T(8,128)(2,1)} %k_hbm.1, bf16[256,640]{1,0:T(8,128)(2,1)} %v_hbm.1, s32[256,128]{1,0:T(8,128)} %bitcast.3, s32[128,128]{1,0:T(8,128)} %mask_hbm.1, bf16[256,1280]{1,0:T(8,128)(2,1)} %tok_hbm.1, bf16[640,1280]{1,0:T(8,128)(2,1)} %w_hbm.1, ...), custom_call_target="tpu_custom_call" | custom-call | tf_op jit(solution)/shard_map/pallas_call | solution.py:414
  157.4 2.5 %copy.11 = bf16[128,5120]{1,0:T(8,128)(2,1)} copy(bf16[128,5120]{1,0:T(8,128)(2,1)} %shard_map.91) | data formatting | bytes 2621440

commit v7 on v6

--- a/solution.py
+++ b/solution.py
@@ -13,7 +13,7 @@
 LANES = 128
 PLANE = 8
 REACH = 4
-CHUNKS = 5
+CHUNKS = 8
 PARTS = 2
 
 

time: 161 us -> 160 us (level)
  no operation moved by 1% of the time
where the time goes in v7:
time: 160 us; the launch traced here: 159 us
  Pallas kernels  156 us (98%)
  local copies, waits for them, and re-layouts  2.46 us (2%)
    pallas_call x1, Pallas kernels, per_device(): pl.pallas_call(program_kernel, out_shape=jax.ShapeDtypeStruct((capacity,...  156 us

profile of v7, /device:TPU:24, one launch (start us, length us, event | category | flops | bytes accessed | tf_op | source)
XLA Modules:
  0.0 158.6 jit_solution(16876101310680691501)
XLA Ops:
  0.0 156.1 %shard_map.91 = bf16[128,5120]{1,0:T(8,128)(2,1)} custom-call(bf16[256,640]{1,0:T(8,128)(2,1)} %q_hbm.1, bf16[256,640]{1,0:T(8,128)(2,1)} %k_hbm.1, bf16[256,640]{1,0:T(8,128)(2,1)} %v_hbm.1, s32[256,128]{1,0:T(8,128)} %bitcast.3, s32[128,128]{1,0:T(8,128)} %mask_hbm.1, bf16[256,1280]{1,0:T(8,128)(2,1)} %tok_hbm.1, bf16[640,1280]{1,0:T(8,128)(2,1)} %w_hbm.1, ...), custom_call_target="tpu_custom_call" | custom-call | tf_op jit(solution)/shard_map/pallas_call | solution.py:414
  156.1 2.5 %copy.11 = bf16[128,5120]{1,0:T(8,128)(2,1)} copy(bf16[128,5120]{1,0:T(8,128)(2,1)} %shard_map.91) | data formatting | bytes 2621440
